TPU v7x, 32 devices: a whole 2x2x4 slice. The times are simulated.
32 devices in a mesh: mp: 8 (over z, x), station: 4 (over y, core).
Axes of the slice: x: 2, y: 2, z: 4, core: 2. Of those that a mesh axis runs over, the one named last changes fastest.
Arguments:
- p_now: float32 [64, 64, 128], P('mp'), may hold values from -2.7 to 2.7
- p_prev: float32 [64, 64, 128], P('mp'), may hold values from -2.7 to 2.7
- velocity: float32 [64, 64, 128], P('mp'), may hold values from 4 to 4.5
- density: float32 [64, 64, 128], P('mp'), may hold values from -6 to 6
- wavelet: float32 [16], replicated, may hold values from -4 to 4
- source_cell: int32 [1], replicated, may hold values from 0 to 524287
- receiver_cells: int32 [256], replicated, may hold values from 0 to 4095
- station_cells: int32 [512], P('station'), may hold values from 0 to 4095
- observed: float32 [512], P('station'), may hold values from -6 to 6
Outputs:
- wavefield: float32 [64, 64, 128], P('mp')
- traces: float32 [16, 256], replicated
- gravity_residual: float32 [512], P('station')
- density_gradient: float32 [64, 64, 128], P('mp', 'station')
- cross_gradient: float32 [3, 64, 64, 128], P(None, 'mp')
All inputs are finite; a program needn't handle non-finite values.
Results may differ from a plain program's by a relative error of at most 0.0036.
The roundings to bfloat16 on the way count: a program that leaves them out, or rounds other values in their place, can miss the bound.
Values sent between devices are 32-bit elements; how exact they have to be, the bound alone decides.
No kernel may reach another device: no remote copies, remote signals or barrier semaphores. Data moves between devices by JAX's collectives and lax.ppermute only.
A program may use at most 64 MiB of HBM per device.

v0:
```python
import functools

import jax
import jax.numpy as jnp
from jax import lax
from jax.experimental import pallas as pl
from jax.experimental.pallas import tpu as pltpu
from jax.sharding import PartitionSpec as P


STENCIL = (-205.0 / 72.0, 8.0 / 5.0, -1.0 / 5.0, 8.0 / 315.0, -1.0 / 560.0)
TIME_RATIO = 0.1
REACH = 4
AXES = ("mp", "station")
VMEM = pl.BlockSpec(memory_space=pltpu.VMEM)
SMEM = pl.BlockSpec(memory_space=pltpu.SMEM)
HBM = pl.BlockSpec(memory_space=pltpu.HBM)
F32 = jnp.float32
MIB = 1 << 20


def room(mib):
    return pltpu.CompilerParams(vmem_limit_bytes=mib * MIB)


def shape(dims):
    return jax.ShapeDtypeStruct(dims, F32)


def pairs_of(count, stations, partner):
    return [
        (m * stations + s, (lambda t: t[0] * stations + t[1])(partner(m, s)))
        for m in range(count)
        for s in range(stations)
    ]


def chain_partner(count):
    def partner(m, s):
        if s % 2 == 0:
            return (m ^ 1, s)
        other = m + 1 if m % 2 else m - 1
        if other < 0 or other >= count:
            return (m, s ^ 2)
        return (other, s)

    return partner


def position():
    m = lax.axis_index("mp")
    return m, (m + lax.axis_index("station")) % 2 == 0


def divmod_static(value, divisor):
    if divisor & (divisor - 1) == 0:
        return value >> (divisor.bit_length() - 1), value & (divisor - 1)
    return value // divisor, value % divisor


def in_place(*values):
    return [pltpu.with_memory_space_constraint(value, pltpu.HBM) for value in values]


def run_copies(pairs, sems):
    copies = [pltpu.make_async_copy(a, b, sems.at[i]) for i, (a, b) in enumerate(pairs)]
    for copy in copies:
        copy.start()
    for copy in copies:
        copy.wait()


def plane_of(upper, j, slab):
    return jnp.where(upper, slab - 1 - j, j)


def first_kernel(now, cur, sems):
    slab = now.shape[0]
    _, upper = position()
    run_copies([(now.at[plane_of(upper, j, slab)], cur.at[j]) for j in range(slab // 2)], sems)


def first_planes(p_now):
    slab, rows, lanes = p_now.shape
    half = slab // 2
    return pl.pallas_call(
        first_kernel,
        out_shape=shape((half, rows, lanes)),
        in_specs=[HBM],
        out_specs=VMEM,
        scratch_shapes=[pltpu.SemaphoreType.DMA((half,))],
        compiler_params=room(2),
        name="first_planes",
    )(*in_place(p_now))


def setup_kernel(
    count,
    source,
    wavelet_in,
    cells_in,
    observed,
    p_prev,
    velocity,
    density,
    prev,
    cour,
    cour_outer,
    mask,
    dens,
    pulses,
    known,
    edges,
    vel,
    raw,
    wavelet,
    cells,
    sems,
):
    slab = p_prev.shape[0]
    half, rows, lanes = prev.shape
    m, upper = position()
    pairs = []
    for j in range(half):
        plane = plane_of(upper, j, slab)
        pairs += [(p_prev.at[plane], prev.at[j]), (velocity.at[plane], vel.at[j])]
    low = half * (lax.axis_index("station") % 2)
    pairs += [(density.at[pl.ds(low, half)], raw)]
    edge = plane_of(upper, 0, slab)
    pairs += [(velocity.at[edge], edges.at[0]), (density.at[edge], edges.at[1])]
    pairs += [(wavelet_in, wavelet), (cells_in, cells), (observed, known.at[1])]
    run_copies(pairs, sems)
    known[0] = cells[...].astype(F32)
    for n in range(pulses.shape[0]):
        pulses[n : n + 1, :] = jnp.full((1, lanes), wavelet[n], F32)
    outer_ok = jnp.where(upper, m < count - 1, m > 0)
    outer_ok = jnp.where(outer_ok, 1.0, 0.0)
    column, source_lane = divmod_static(source[0], lanes)
    source_x, source_row = divmod_static(column, rows)
    row = lax.broadcasted_iota(jnp.int32, (rows, lanes), 0)
    lane = lax.broadcasted_iota(jnp.int32, (rows, lanes), 1)
    spot = jnp.where((row == source_row) & (lane == source_lane), 1.0, 0.0)
    for j in range(half):
        scaled = TIME_RATIO * vel[j]
        square = scaled * scaled
        cour[j] = square
        cour_outer[j] = square * outer_ok
        here = m * slab + plane_of(upper, j, slab) == source_x
        mask[j] = spot * jnp.where(here, 1.0, 0.0)
        dens[j] = raw[j].astype(jnp.bfloat16).astype(F32)


def setup(count, source_cell, wavelet, cells, observed, p_prev, velocity, density):
    slab, rows, lanes = p_prev.shape
    half = slab // 2
    part = shape((half, rows, lanes))
    held = pltpu.VMEM((half, rows, lanes), F32)
    return pl.pallas_call(
        functools.partial(setup_kernel, count),
        out_shape=(part,) * 5
        + (
            shape((wavelet.shape[0], lanes)),
            shape((2,) + cells.shape),
            shape((2, rows, lanes)),
        ),
        in_specs=[SMEM] + [HBM] * 6,
        out_specs=(VMEM,) * 8,
        scratch_shapes=[
            held,
            held,
            pltpu.SMEM(wavelet.shape, F32),
            pltpu.VMEM(cells.shape, jnp.int32),
            pltpu.SemaphoreType.DMA((2 * half + 6,)),
        ],
        compiler_params=room(4),
        cost_estimate=pl.CostEstimate(
            flops=20 * half * rows * lanes, bytes_accessed=32 * half * rows * lanes, transcendentals=0
        ),
        name="setup",
    )(source_cell, *in_place(wavelet, cells, observed, p_prev, velocity, density))


def local_kernel(step, pulses, mask, cur, prev, cour, surf_in, base, surf, pad):
    planes, rows, lanes = prev.shape
    lane = lax.broadcasted_iota(jnp.int32, (rows, lanes), 1)
    weights = {}
    for d in range(1, REACH + 1):
        weights[d] = jnp.where(lane >= d, STENCIL[d], 0.0)
        weights[-d] = jnp.where(lane < lanes - d, STENCIL[d], 0.0)
    pulse = pulses[step : step + 1, :]
    for j in range(planes):
        pad[j, 0:8, :] = jnp.zeros((8, lanes), F32)
        pad[j, 8 + rows : 16 + rows, :] = jnp.zeros((8, lanes), F32)
        pad[j, 8 : 8 + rows, :] = cur[j]
    for j in range(planes):
        c = cur[j]
        acc = 3.0 * STENCIL[0] * c
        for d in range(1, REACH + 1):
            acc = acc + weights[d] * pltpu.roll(c, d, 1) + weights[-d] * pltpu.roll(c, lanes - d, 1)
            near = pad[j, 8 + d : 8 + d + rows, :] + pad[j, 8 - d : 8 - d + rows, :]
            for i in (j - d, j + d):
                if 0 <= i < planes:
                    near = near + cur[i]
            acc = acc + STENCIL[d] * near
        base[j] = 2.0 * c - prev[j] + cour[j] * acc + pulse * mask[j]
        if step == 0:
            surf[j] = jnp.zeros((rows, lanes), F32)
        else:
            surf[j] = jnp.where(
                lane == step - 1, jnp.broadcast_to(c[:, 0:1], (rows, lanes)), surf_in[j]
            )


def local_step(step, pulses, mask, cur, prev, cour, surf):
    planes, rows, lanes = cur.shape
    return pl.pallas_call(
        functools.partial(local_kernel, step),
        out_shape=(shape(cur.shape), shape(cur.shape)),
        in_specs=[VMEM] * 6,
        out_specs=(VMEM, VMEM),
        scratch_shapes=[pltpu.VMEM((planes, rows + 16, lanes), F32)],
        compiler_params=room(2),
        cost_estimate=pl.CostEstimate(
            flops=60 * cur.size, bytes_accessed=24 * cur.size, transcendentals=0
        ),
        name="wave_local",
    )(pulses, mask, cur, prev, cour, surf)


def halo_kernel(base, cour, cour_outer, outer, inner, out):
    planes = base.shape[0]
    for j in range(planes):
        far = near = None
        for d in range(j + 1, REACH + 1):
            term = STENCIL[d] * outer[d - j - 1]
            far = term if far is None else far + term
        for d in range(planes - j, REACH + 1):
            term = STENCIL[d] * inner[2 * planes - 1 - j - d]
            near = term if near is None else near + term
        out[j] = base[j] + (cour[j] * near + cour_outer[j] * far)


def halo_step(base, cour, cour_outer, outer, inner):
    return pl.pallas_call(
        halo_kernel,
        out_shape=shape(base.shape),
        in_specs=[VMEM] * 5,
        out_specs=VMEM,
        compiler_params=room(2),
        cost_estimate=pl.CostEstimate(
            flops=12 * base.size, bytes_accessed=20 * base.size, transcendentals=0
        ),
        name="wave_halo",
    )(base, cour, cour_outer, outer, inner)


def trace_kernel(step, place, cur, surf, out):
    planes, rows, lanes = cur.shape
    receivers = place.shape[1]
    steps = step + 1
    lane = lax.broadcasted_iota(jnp.int32, (rows, lanes), 1)
    columns = jnp.concatenate(
        [
            jnp.where(lane == step, jnp.broadcast_to(cur[j, :, 0:1], (rows, lanes)), surf[j])
            for j in range(planes)
        ],
        0,
    )
    columns = columns.T
    spot = lax.broadcasted_iota(jnp.int32, (planes * rows, receivers), 0)
    pick = jnp.where(place[...] == spot, 1.0, 0.0).astype(jnp.bfloat16)
    total = None
    for _ in range(3):
        part = columns.astype(jnp.bfloat16)
        columns = columns - part.astype(F32)
        term = jnp.dot(part, pick, preferred_element_type=F32)
        total = term if total is None else total + term
    for b in range(receivers // 128):
        out[b * steps : (b + 1) * steps, :] = total[:steps, b * 128 : (b + 1) * 128]


def recorded_traces(step, place, cur, surf):
    return pl.pallas_call(
        functools.partial(trace_kernel, step),
        out_shape=shape(((step + 1) * (place.shape[1] // 128), 128)),
        in_specs=[VMEM] * 3,
        out_specs=VMEM,
        compiler_params=room(4),
        name="traces",
    )(place, cur, surf)


def join_kernel(own, sibling, out, sems):
    slab = out.shape[0]
    _, upper = position()
    pairs = []
    for j in range(slab // 2):
        here = plane_of(upper, j, slab)
        pairs += [(own.at[j], out.at[here]), (sibling.at[j], out.at[slab - 1 - here])]
    run_copies(pairs, sems)


def join(own, sibling):
    half, rows, lanes = own.shape
    return pl.pallas_call(
        join_kernel,
        out_shape=shape((2 * half, rows, lanes)),
        in_specs=[VMEM] * 2,
        out_specs=HBM,
        scratch_shapes=[pltpu.SemaphoreType.DMA((2 * half,))],
        compiler_params=room(2),
        name="join",
    )(own, sibling)


def on_chip(value):
    return pltpu.with_memory_space_constraint(value, pltpu.VMEM)


def table_low(total_x, slab, offset):
    m, _ = position()
    return m * slab - (total_x - 1) + offset


def table_kernel(total_x, slab, spread, head, out):
    lanes = out.shape[1]
    low = table_low(total_x, slab, head[0])
    dy = (lax.broadcasted_iota(jnp.int32, (spread, lanes), 0) - (spread // 2 - 1)).astype(F32)
    dz = (lax.broadcasted_iota(jnp.int32, (spread, lanes), 1) + 1).astype(F32)
    side = dy * dy
    deep = dz * dz

    def one(t, carry):
        dx = (t + low).astype(F32)
        inverse = lax.rsqrt(dx * dx + side + deep)
        value = dz * (inverse * inverse * inverse)
        start = pl.multiple_of(t * spread, spread)
        out[pl.ds(start, spread), :] = value.astype(jnp.bfloat16).astype(F32)
        return carry

    lax.fori_loop(0, out.shape[0] // spread, one, 0)


def gravity_table(total_x, slab, depth, lateral, vertical, head):
    size = depth * 2 * lateral * vertical
    return pl.pallas_call(
        functools.partial(table_kernel, total_x, slab, 2 * lateral),
        out_shape=shape((depth * 2 * lateral, vertical)),
        in_specs=[SMEM],
        out_specs=VMEM,
        cost_estimate=pl.CostEstimate(
            flops=20 * size, bytes_accessed=4 * size, transcendentals=2 * size
        ),
        compiler_params=room(8),
        name="gravity_table",
    )(head)


def forward_kernel(first, guard, total_x, lateral, head, table, dens, out):
    planes, rows, _ = dens.shape
    count = out.shape[0]
    spread = 2 * lateral
    core = lax.axis_index("station") % 2
    lead = total_x - 1 - head[0]
    if guard:
        out[...] = jnp.zeros_like(out)

    def one(s, carry):
        sx, sy = divmod_static(head[1 + first + s], lateral)
        shift = lead - sx
        start = (shift + core * planes) * spread + (lateral - 1 - sy)

        def accumulate():
            acc = None
            for p in range(planes):
                term = table[pl.ds(start + p * spread, rows), :] * dens[p]
                acc = term if acc is None else acc + term
            out[pl.ds(s, 1), :] = jnp.sum(acc, axis=0, keepdims=True)

        if guard:
            pl.when((shift >= 0) & (shift < guard))(accumulate)
        else:
            accumulate()
        return carry

    lax.fori_loop(0, count, one, 0, unroll=8)


def gravity_forward(first, count, guard, total_x, lateral, head, table, dens):
    work = count * dens.size
    return pl.pallas_call(
        functools.partial(forward_kernel, first, guard, total_x, lateral),
        out_shape=shape((count, dens.shape[2])),
        in_specs=[SMEM, VMEM, VMEM],
        out_specs=VMEM,
        cost_estimate=pl.CostEstimate(
            flops=4 * work, bytes_accessed=4 * dens.size, transcendentals=0
        ),
        compiler_params=room(8),
        name="gravity_forward",
    )(head, on_chip(table), dens)


def adjoint_kernel(lines, guard, total_x, lateral, head, weights, table, start_at, out):
    slab, rows, _ = out.shape
    spread = 2 * lateral
    lead = total_x - 1 - head[0]
    row_low = lax.axis_index("station") * rows

    def one(k, i, acc):
        sx, sy = divmod_static(head[1 + 128 * k + i], lateral)
        shift = lead - sx
        weight = weights[k, i]
        if guard:
            keep = (shift >= 0) & (shift < guard)
            shift = jnp.where(keep, shift, 0)
            weight = jnp.where(keep, weight, 0.0)
        start = shift * spread + (lateral - 1 - sy + row_low)
        return tuple(
            acc[x] + weight * table[pl.ds(start + x * spread, rows), :] for x in range(slab)
        )

    acc = tuple(start_at[x] for x in range(slab))
    for k in lines:
        acc = lax.fori_loop(0, 128, functools.partial(one, k), acc, unroll=16)
    for x in range(slab):
        out[x] = acc[x]


def gravity_adjoint(lines, guard, total_x, lateral, head, weights, table, start_at):
    return pl.pallas_call(
        functools.partial(adjoint_kernel, lines, guard, total_x, lateral),
        out_shape=shape(start_at.shape),
        in_specs=[SMEM, SMEM, VMEM, VMEM],
        out_specs=VMEM,
        cost_estimate=pl.CostEstimate(
            flops=256 * len(lines) * start_at.size, bytes_accessed=8 * start_at.size, transcendentals=0
        ),
        compiler_params=room(8),
        name="gravity_adjoint",
    )(head, weights, table, start_at)


def small_call(kernel, outs, *values):
    single = not isinstance(outs, tuple)
    return pl.pallas_call(
        kernel,
        out_shape=outs,
        in_specs=[VMEM] * len(values),
        out_specs=VMEM if single else (VMEM,) * len(outs),
        compiler_params=room(2),
    )(*values)


def sum_kernel(first, second, out):
    out[...] = first[...] + second[...]


def plus(first, second):
    return small_call(sum_kernel, shape(first.shape), first, second)


def unpack_kernel(packed, other, out):
    steps, receivers = out.shape
    for b in range(receivers // 128):
        rows = slice(b * steps, (b + 1) * steps)
        out[:, b * 128 : (b + 1) * 128] = packed[rows, :] + other[rows, :]


def predict_kernel(*refs):
    pieces, out = refs[:-1], refs[-1]
    sums = jnp.concatenate([piece[...] for piece in pieces], 0)
    for k in range(out.shape[0]):
        out[k : k + 1, :] = jnp.sum(sums[k * 128 : (k + 1) * 128, :].T, axis=0, keepdims=True)


def residual_kernel(packed, other, observed, weights, own):
    residual = packed[...] + other[...] - observed[...]
    weights[...] = residual.astype(jnp.bfloat16).astype(F32)
    mine = own.shape[0]
    for k in range(residual.shape[0] // mine):

        @pl.when(lax.axis_index("station") == k)
        def _(k=k):
            own[...] = residual[k * mine : (k + 1) * mine, :]


def cross_kernel(count, velocity, density, outer, inner, out):
    slab, rows, lanes = velocity.shape
    lane = lax.broadcasted_iota(jnp.int32, (rows, lanes), 1)
    row = lax.broadcasted_iota(jnp.int32, (rows, lanes), 0)
    m, flipped = position()
    left_ok = jnp.where(m > 0, 0.5, 0.0)
    right_ok = jnp.where(m < count - 1, 0.5, 0.0)

    def slopes(field, side, x):
        f = field[x]
        if x > 0:
            below = 0.5 * field[x - 1]
        else:
            below = left_ok * jnp.where(flipped, inner[side], outer[side])
        if x < slab - 1:
            above = 0.5 * field[x + 1]
        else:
            above = right_ok * jnp.where(flipped, outer[side], inner[side])
        up = jnp.where(row < rows - 1, pltpu.roll(f, rows - 1, 0), 0.0)
        down = jnp.where(row > 0, pltpu.roll(f, 1, 0), 0.0)
        ahead = jnp.where(lane < lanes - 1, pltpu.roll(f, lanes - 1, 1), 0.0)
        back = jnp.where(lane > 0, pltpu.roll(f, 1, 1), 0.0)
        return above - below, (up - down) * 0.5, (ahead - back) * 0.5

    for x in range(slab):
        v = slopes(velocity, 0, x)
        q = slopes(density, 1, x)
        out[0, x] = v[1] * q[2] - v[2] * q[1]
        out[1, x] = v[2] * q[0] - v[0] * q[2]
        out[2, x] = v[0] * q[1] - v[1] * q[0]


def cross_gradient_of(count, velocity, density, outer, inner):
    return pl.pallas_call(
        functools.partial(cross_kernel, count),
        out_shape=shape((3,) + velocity.shape),
        in_specs=[VMEM] * 4,
        out_specs=VMEM,
        cost_estimate=pl.CostEstimate(
            flops=60 * velocity.size, bytes_accessed=24 * velocity.size, transcendentals=0
        ),
        compiler_params=room(8),
        name="cross_gradient",
    )(velocity, density, outer, inner)


def per_device(
    p_now, p_prev, velocity, density, wavelet, source_cell, receiver_cells, station_cells, observed
):
    slab, lateral, vertical = p_now.shape
    count = lax.axis_size("mp")
    stations = lax.axis_size("station")
    steps = wavelet.shape[0]
    half = slab // 2
    assert half == REACH and count % 2 == 0 and stations % 4 == 0
    total_x = slab * count
    m, upper = position()
    s = lax.axis_index("station")
    block = lateral // stations
    chain = pairs_of(count, stations, chain_partner(count))
    together = lax.optimization_barrier

    def across(value):
        return lax.ppermute(value, AXES, chain)

    def swap(value, slab_bit, station_bit):
        pairs = pairs_of(count, stations, lambda i, k: (i ^ slab_bit, k ^ station_bit))
        return lax.ppermute(value, AXES, pairs)

    cur = first_planes(p_now)
    outer = across(cur)
    inner = swap(cur, 0, 1)
    prev, cour, cour_outer, mask, dens, pulses, known, edges = setup(
        count,
        source_cell,
        wavelet,
        station_cells.reshape(-1, 128),
        observed.reshape(-1, 128),
        p_prev,
        velocity,
        density,
    )

    receiver_x, receiver_y = divmod_static(receiver_cells, lateral)
    receiver_j = receiver_x - m * slab
    receiver_j = jnp.where(upper, slab - 1 - receiver_j, receiver_j)
    inside = (receiver_j >= 0) & (receiver_j < half)
    place = jnp.where(inside, receiver_j * lateral + receiver_y, -1)[None, :]

    reach = min(total_x, 64)
    chunks = -(-total_x // reach)
    span = reach + slab - 1
    own_stations = station_cells.shape[0]
    n_stations = own_stations * stations

    def head_of(offset, cells):
        return jnp.concatenate([jnp.reshape(offset, (1,)).astype(jnp.int32), cells])

    def table_of(head):
        return gravity_table(total_x, slab, span, lateral, vertical, head)

    state = {"known": known, "edges": edges}

    def merged(gate):
        if "pending" not in state:
            return gate(state["known"])
        known, other, bit = state.pop("pending")
        other = gate(other)
        upper = (s // bit) % 2 == 1
        pair = [jnp.where(upper, other, known), jnp.where(upper, known, other)]
        state["known"] = jnp.concatenate(pair, 1)
        return state["known"]

    def exchange(bit):
        def work(gate):
            known = merged(gate)
            state["pending"] = known, swap(known, 0, bit), bit

        return work

    def send_edges(gate):
        state["outer"] = across(gate(state["edges"]))

    def share_edges(gate):
        state["inner"] = swap(gate(state["outer"]), 0, 1)

    def cross(gate):
        state["cross"] = cross_gradient_of(
            count, velocity, density, state["outer"], gate(state["inner"])
        )
        return "cross"

    lines = n_stations // 128

    def build_table(gate):
        known = merged(gate)
        cells = known[0].reshape(-1).astype(jnp.int32)
        head = head_of(0, cells)
        zero, head, observed_all, where = together(
            (jnp.zeros((1,), jnp.int32), head, known[1].reshape(-1, 128), place)
        )
        state.update(head=head, observed=observed_all, place=where)
        state["table"] = table_of(zero)
        return "table"

    pieces = 5
    part = -(-n_stations // (8 * pieces)) * 8

    def forward(i):
        def work(gate):
            size = min(part, n_stations - i * part)
            state[i] = gravity_forward(
                i * part, size, 0, total_x, lateral, gate(state["head"]), state["table"], dens
            )
            return i

        return work

    def predict(gate):
        sums = [state[i] for i in range(pieces)]
        sums[0] = gate(sums[0])
        packed = small_call(predict_kernel, shape((lines, 128)), *sums)
        state["packed"], state["other"] = packed, swap(packed, 0, 1)

    def add_up(bit):
        def work(gate):
            packed = plus(gate(state["packed"]), state["other"])
            state["packed"], state["other"] = packed, swap(packed, bit, 1)

        return work

    def residual(gate):
        state["weights"], state["own"] = small_call(
            residual_kernel,
            (shape((lines, 128)), shape((lines // stations, 128))),
            gate(state["packed"]),
            state["other"],
            state["observed"],
        )
        state["gradient"] = jnp.zeros((slab, block, vertical), F32)
        return "weights"

    def adjoint(half_lines):
        def work(gate):
            state["gradient"] = gravity_adjoint(
                half_lines,
                0,
                total_x,
                lateral,
                state["head"],
                gate(state["weights"]),
                state["table"],
                state["gradient"],
            )
            return "gradient"

        return work

    def both(first, second):
        def work(gate):
            first(gate)
            return second(gate)

        return work

    hidden = chunks == 1 and count & (count - 1) == 0
    jobs = [exchange(1 << b) for b in range(stations.bit_length() - 1)]
    if hidden:
        jobs += [build_table] + [forward(i) for i in range(pieces)] + [both(predict, cross)]
        jobs += [add_up(1 << b) for b in range(count.bit_length() - 1)] + [residual]
        jobs += [adjoint(range(lines // 2)), adjoint(range(lines // 2, lines))]
    jobs[0] = both(send_edges, jobs[0])
    jobs[1] = both(share_edges, jobs[1])
    if not hidden:
        jobs.append(cross)
    assert len(jobs) < steps

    surf = cour
    for step in range(steps):
        if step:
            outer = across(cur)
            inner = swap(cur, 0, 1)
        base, surf = local_step(step, pulses, mask, cur, prev, cour, surf)

        def gate(value):
            nonlocal base
            base, value = together((base, value))
            return value

        ready = None
        if step and jobs:
            ready = jobs.pop(0)(gate)
        cur, prev = halo_step(base, cour, cour_outer, outer, inner), cur
        if ready is not None:
            cur, state[ready] = together((cur, state[ready]))

    sibling = swap(cur, 0, 1)
    packed = recorded_traces(steps - 1, state.get("place", place), cur, surf)
    other = swap(packed, 0, 1)
    if count & (count - 1) == 0:
        bit = 1
        while bit < count:
            packed = plus(packed, other)
            other = swap(packed, bit, 1)
            if bit == 1:
                wavefield = join(cur, sibling)
            if bit == 2:
                other, wavefield = together((other, wavefield))
            bit *= 2
    else:
        wavefield = join(cur, sibling)
        packed = lax.psum(packed + other, "mp")
        other = jnp.zeros_like(packed)
    traces = small_call(unpack_kernel, shape((steps, receiver_cells.shape[0])), packed, other)
    if hidden:
        gravity_residual = state["own"].reshape(-1)
        density_gradient = state["gradient"]
    else:
        known = merged(lambda value: value)
        cells = known[0].reshape(-1).astype(jnp.int32)

        def add_chunk(i, total):
            head = head_of(i * reach, cells)
            return total + gravity_forward(
                0, n_stations, reach, total_x, lateral, head, table_of(head[:1]), dens
            )

        sums = lax.fori_loop(0, chunks, add_chunk, jnp.zeros((n_stations, vertical), F32))
        predicted = jnp.sum(sums, axis=1)
        predicted = lax.psum(predicted + swap(predicted, 0, 1), "mp")
        difference = predicted - known[1].reshape(-1)
        gravity_residual = lax.dynamic_slice(difference, (s * own_stations,), (own_stations,))
        weights = difference.astype(jnp.bfloat16).astype(F32).reshape(-1, 128)

        def back_chunk(i, total):
            head = head_of(i * reach, cells)
            return gravity_adjoint(
                range(lines), reach, total_x, lateral, head, weights, table_of(head[:1]), total
            )

        density_gradient = lax.fori_loop(
            0, chunks, back_chunk, jnp.zeros((slab, block, vertical), F32)
        )
    return (wavefield, traces, gravity_residual, density_gradient, state["cross"])


def solution(mesh):
    in_specs = (
        P("mp", None, None),
        P("mp", None, None),
        P("mp", None, None),
        P("mp", None, None),
        P(),
        P(),
        P(),
        P("station"),
        P("station"),
    )
    out_specs = (
        P("mp", None, None),
        P(),
        P("station"),
        P("mp", "station", None),
        P(None, "mp", None, None),
    )

    return jax.shard_map(
        per_device, mesh=mesh, in_specs=in_specs, out_specs=out_specs, check_vma=False
    )
```

profile of v0, /device:TPU:0, one launch (start us, length us, event | category | flops | bytes accessed | tf_op | source)
XLA Modules:
  0.0 107.3 jit_solution(17956973298190643912)
XLA Ops:
  1.5 3.0 %collective-permute-start = (f32[4,64,128]{2,1,0:T(8,128)S(1)}, f32[4,64,128]{2,1,0:T(8,128)S(1)}, u32[]{:S(2)}, u32[]{:S(2)}) collective-permute-start(f32[4,64,128]{2,1,0:T(8,128)S(1)} %first_planes.1.cur.prev), channel_id=1, source_target_pairs={{0,4},{1,3},{2,6},{3,1},{4,0},{5,9},{6,2},{7,11},{8,12},{9,5},{10,... | collective-permute-start | bytes 393224 | tf_op jit(solution)/shard_map/ppermute | solution.py:551
  8.3 2.5 %collective-permute-start.2 = (f32[4,64,128]{2,1,0:T(8,128)S(1)}, f32[4,64,128]{2,1,0:T(8,128)S(1)}, u32[]{:S(2)}, u32[]{:S(2)}) collective-permute-start(f32[4,64,128]{2,1,0:T(8,128)S(1)} %wave_halo.16.cur.prev), channel_id=1, source_target_pairs={{0,4},{1,3},{2,6},{3,1},{4,0},{5,9},{6,2},{7,11},{8,12},{9,5},{10,... | collective-permute-start | bytes 393224 | tf_op jit(solution)/shard_map/ppermute | solution.py:551
  11.4 1.7 %collective-permute-start.5 = (f32[2,1,128]{2,1,0:T(1,128)S(1)}, f32[2,1,128]{2,1,0:T(1,128)S(1)}, u32[]{:S(2)}, u32[]{:S(2)}) collective-permute-start(f32[2,1,128]{2,1,0:T(1,128)S(1)} %get-tuple-element.125), channel_id=1, source_target_pairs={{0,1},{1,0},{2,3},{3,2},{4,5},{5,4},{6,7},{7,6},{8,9},{9,8},{10,11... | collective-permute-start | bytes 3080 | tf_op jit(solution)/shard_map/ppermute | solution.py:555
  13.8 2.1 %collective-permute-start.6 = (f32[4,64,128]{2,1,0:T(8,128)S(1)}, f32[4,64,128]{2,1,0:T(8,128)S(1)}, u32[]{:S(2)}, u32[]{:S(2)}) collective-permute-start(f32[4,64,128]{2,1,0:T(8,128)S(1)} %wave_halo.17.cur.prev), channel_id=1, source_target_pairs={{0,4},{1,3},{2,6},{3,1},{4,0},{5,9},{6,2},{7,11},{8,12},{9,5},{10,... | collective-permute-start | bytes 393224 | tf_op jit(solution)/shard_map/ppermute | solution.py:551
  19.0 2.2 %collective-permute-start.9 = (f32[4,64,128]{2,1,0:T(8,128)S(1)}, f32[4,64,128]{2,1,0:T(8,128)S(1)}, u32[]{:S(2)}, u32[]{:S(2)}) collective-permute-start(f32[4,64,128]{2,1,0:T(8,128)S(1)} %wave_halo.18.cur.prev), channel_id=1, source_target_pairs={{0,4},{1,3},{2,6},{3,1},{4,0},{5,9},{6,2},{7,11},{8,12},{9,5},{10,... | collective-permute-start | bytes 393224 | tf_op jit(solution)/shard_map/ppermute | solution.py:551
  21.7 1.8 %gravity_table.1.table = f32[9088,128]{1,0:T(8,128)S(1)} custom-call(s32[1]{0:T(128)} %constant.54.clone.1.head), custom_call_target="tpu_custom_call" | custom-call | flops 23265280 | bytes 4653056 | tf_op jit(solution)/shard_map/gravity_table/pallas_call | solution.py:346
  25.2 2.5 %collective-permute-start.11 = (f32[4,64,128]{2,1,0:T(8,128)S(1)}, f32[4,64,128]{2,1,0:T(8,128)S(1)}, u32[]{:S(2)}, u32[]{:S(2)}) collective-permute-start(f32[4,64,128]{2,1,0:T(8,128)S(1)} %wave_halo.19.cur.prev), channel_id=1, source_target_pairs={{0,4},{1,3},{2,6},{3,1},{4,0},{5,9},{6,2},{7,11},{8,12},{9,5},{10,... | collective-permute-start | bytes 393224 | tf_op jit(solution)/shard_map/ppermute | solution.py:551
  28.1 1.9 %gravity_forward.5.refs_0_ = f32[104,128]{1,0:T(8,128)S(1)} custom-call(s32[513]{0:T(1024)S(1)} %pad_add_fusion.head, f32[9088,128]{1,0:T(8,128)S(1)} %gravity_table.1.table, f32[4,64,128]{2,1,0:T(8,128)S(1)} %get-tuple-element.141.dens), custom_call_target="tpu_custom_call" | custom-call | flops 13631488 | bytes 131072 | tf_op jit(solution)/shard_map/gravity_forward/pallas_call | solution.py:391
  30.7 2.3 %collective-permute-start.13 = (f32[4,64,128]{2,1,0:T(8,128)S(1)}, f32[4,64,128]{2,1,0:T(8,128)S(1)}, u32[]{:S(2)}, u32[]{:S(2)}) collective-permute-start(f32[4,64,128]{2,1,0:T(8,128)S(1)} %wave_halo.20.cur.prev), channel_id=1, source_target_pairs={{0,4},{1,3},{2,6},{3,1},{4,0},{5,9},{6,2},{7,11},{8,12},{9,5},{10,... | collective-permute-start | bytes 393224 | tf_op jit(solution)/shard_map/ppermute | solution.py:551
  33.4 1.9 %gravity_forward.6.refs_1_ = f32[104,128]{1,0:T(8,128)S(1)} custom-call(s32[513]{0:T(1024)S(1)} %pad_add_fusion.head, f32[9088,128]{1,0:T(8,128)S(1)} %gravity_table.1.table, f32[4,64,128]{2,1,0:T(8,128)S(1)} %get-tuple-element.141.dens), custom_call_target="tpu_custom_call" | custom-call | flops 13631488 | bytes 131072 | tf_op jit(solution)/shard_map/gravity_forward/pallas_call | solution.py:391
  36.0 2.1 %collective-permute-start.15 = (f32[4,64,128]{2,1,0:T(8,128)S(1)}, f32[4,64,128]{2,1,0:T(8,128)S(1)}, u32[]{:S(2)}, u32[]{:S(2)}) collective-permute-start(f32[4,64,128]{2,1,0:T(8,128)S(1)} %wave_halo.21.cur.prev), channel_id=1, source_target_pairs={{0,4},{1,3},{2,6},{3,1},{4,0},{5,9},{6,2},{7,11},{8,12},{9,5},{10,... | collective-permute-start | bytes 393224 | tf_op jit(solution)/shard_map/ppermute | solution.py:551
  38.5 1.9 %gravity_forward.7.refs_2_ = f32[104,128]{1,0:T(8,128)S(1)} custom-call(s32[513]{0:T(1024)S(1)} %pad_add_fusion.head, f32[9088,128]{1,0:T(8,128)S(1)} %gravity_table.1.table, f32[4,64,128]{2,1,0:T(8,128)S(1)} %get-tuple-element.141.dens), custom_call_target="tpu_custom_call" | custom-call | flops 13631488 | bytes 131072 | tf_op jit(solution)/shard_map/gravity_forward/pallas_call | solution.py:391
  41.1 2.1 %collective-permute-start.17 = (f32[4,64,128]{2,1,0:T(8,128)S(1)}, f32[4,64,128]{2,1,0:T(8,128)S(1)}, u32[]{:S(2)}, u32[]{:S(2)}) collective-permute-start(f32[4,64,128]{2,1,0:T(8,128)S(1)} %wave_halo.22.cur.prev), channel_id=1, source_target_pairs={{0,4},{1,3},{2,6},{3,1},{4,0},{5,9},{6,2},{7,11},{8,12},{9,5},{10,... | collective-permute-start | bytes 393224 | tf_op jit(solution)/shard_map/ppermute | solution.py:551
  43.6 1.9 %gravity_forward.8.refs_3_ = f32[104,128]{1,0:T(8,128)S(1)} custom-call(s32[513]{0:T(1024)S(1)} %pad_add_fusion.head, f32[9088,128]{1,0:T(8,128)S(1)} %gravity_table.1.table, f32[4,64,128]{2,1,0:T(8,128)S(1)} %get-tuple-element.141.dens), custom_call_target="tpu_custom_call" | custom-call | flops 13631488 | bytes 131072 | tf_op jit(solution)/shard_map/gravity_forward/pallas_call | solution.py:391
  46.2 2.1 %collective-permute-start.19 = (f32[4,64,128]{2,1,0:T(8,128)S(1)}, f32[4,64,128]{2,1,0:T(8,128)S(1)}, u32[]{:S(2)}, u32[]{:S(2)}) collective-permute-start(f32[4,64,128]{2,1,0:T(8,128)S(1)} %wave_halo.23.cur.prev), channel_id=1, source_target_pairs={{0,4},{1,3},{2,6},{3,1},{4,0},{5,9},{6,2},{7,11},{8,12},{9,5},{10,... | collective-permute-start | bytes 393224 | tf_op jit(solution)/shard_map/ppermute | solution.py:551
  48.7 1.8 %gravity_forward.9.refs_4_ = f32[96,128]{1,0:T(8,128)S(1)} custom-call(s32[513]{0:T(1024)S(1)} %pad_add_fusion.head, f32[9088,128]{1,0:T(8,128)S(1)} %gravity_table.1.table, f32[4,64,128]{2,1,0:T(8,128)S(1)} %get-tuple-element.141.dens), custom_call_target="tpu_custom_call" | custom-call | flops 12582912 | bytes 131072 | tf_op jit(solution)/shard_map/gravity_forward/pallas_call | solution.py:391
  51.3 2.1 %collective-permute-start.22 = (f32[4,64,128]{2,1,0:T(8,128)S(1)}, f32[4,64,128]{2,1,0:T(8,128)S(1)}, u32[]{:S(2)}, u32[]{:S(2)}) collective-permute-start(f32[4,64,128]{2,1,0:T(8,128)S(1)} %wave_halo.24.cur.prev), channel_id=1, source_target_pairs={{0,4},{1,3},{2,6},{3,1},{4,0},{5,9},{6,2},{7,11},{8,12},{9,5},{10,... | collective-permute-start | bytes 393224 | tf_op jit(solution)/shard_map/ppermute | solution.py:551
  56.4 2.1 %collective-permute-start.24 = (f32[4,64,128]{2,1,0:T(8,128)S(1)}, f32[4,64,128]{2,1,0:T(8,128)S(1)}, u32[]{:S(2)}, u32[]{:S(2)}) collective-permute-start(f32[4,64,128]{2,1,0:T(8,128)S(1)} %wave_halo.25.cur.prev), channel_id=1, source_target_pairs={{0,4},{1,3},{2,6},{3,1},{4,0},{5,9},{6,2},{7,11},{8,12},{9,5},{10,... | collective-permute-start | bytes 393224 | tf_op jit(solution)/shard_map/ppermute | solution.py:551
  59.1 2.4 %collective-permute-done.24.outer = f32[4,64,128]{2,1,0:T(8,128)S(1)} collective-permute-done((f32[4,64,128]{2,1,0:T(8,128)S(1)}, f32[4,64,128]{2,1,0:T(8,128)S(1)}, u32[]{:S(2)}, u32[]{:S(2)}) %collective-permute-start.24) | collective-permute-done | bytes 131104 | tf_op jit(solution)/shard_map/ppermute | solution.py:551
  61.5 2.3 %collective-permute-start.27 = (f32[4,64,128]{2,1,0:T(8,128)S(1)}, f32[4,64,128]{2,1,0:T(8,128)S(1)}, u32[]{:S(2)}, u32[]{:S(2)}) collective-permute-start(f32[4,64,128]{2,1,0:T(8,128)S(1)} %wave_halo.26.cur.prev), channel_id=1, source_target_pairs={{0,4},{1,3},{2,6},{3,1},{4,0},{5,9},{6,2},{7,11},{8,12},{9,5},{10,... | collective-permute-start | bytes 393224 | tf_op jit(solution)/shard_map/ppermute | solution.py:551
  66.9 2.1 %collective-permute-start.30 = (f32[4,64,128]{2,1,0:T(8,128)S(1)}, f32[4,64,128]{2,1,0:T(8,128)S(1)}, u32[]{:S(2)}, u32[]{:S(2)}) collective-permute-start(f32[4,64,128]{2,1,0:T(8,128)S(1)} %wave_halo.27.cur.prev), channel_id=1, source_target_pairs={{0,4},{1,3},{2,6},{3,1},{4,0},{5,9},{6,2},{7,11},{8,12},{9,5},{10,... | collective-permute-start | bytes 393224 | tf_op jit(solution)/shard_map/ppermute | solution.py:551
  69.2 2.8 %collective-permute-done.29.second = f32[4,128]{1,0:T(4,128)S(1)} collective-permute-done((f32[4,128]{1,0:T(4,128)S(1)}, f32[4,128]{1,0:T(4,128)S(1)}, u32[]{:S(2)}, u32[]{:S(2)}) %collective-permute-start.29) | collective-permute-done | bytes 2080 | tf_op jit(solution)/shard_map/ppermute | solution.py:555
  74.3 1.9 %collective-permute-start.32 = (f32[4,128]{1,0:T(4,128)S(1)}, f32[4,128]{1,0:T(4,128)S(1)}, u32[]{:S(2)}, u32[]{:S(2)}) collective-permute-start(f32[4,128]{1,0:T(4,128)S(1)} %shard_map.130.first), channel_id=1, source_target_pairs={{0,9},{1,8},{2,11},{3,10},{4,13},{5,12},{6,15},{7,14},{8,1},{9,0},... | collective-permute-start | bytes 6152 | tf_op jit(solution)/shard_map/ppermute | solution.py:555
  76.2 2.0 %collective-permute-done.32.second = f32[4,128]{1,0:T(4,128)S(1)} collective-permute-done((f32[4,128]{1,0:T(4,128)S(1)}, f32[4,128]{1,0:T(4,128)S(1)}, u32[]{:S(2)}, u32[]{:S(2)}) %collective-permute-start.32) | collective-permute-done | bytes 2080 | tf_op jit(solution)/shard_map/ppermute | solution.py:555
  78.2 2.3 %collective-permute-start.35 = (f32[4,128]{1,0:T(4,128)S(1)}, f32[4,128]{1,0:T(4,128)S(1)}, u32[]{:S(2)}, u32[]{:S(2)}) collective-permute-start(f32[4,128]{1,0:T(4,128)S(1)} %shard_map.131.packed), channel_id=1, source_target_pairs={{0,17},{1,16},{2,19},{3,18},{4,21},{5,20},{6,23},{7,22},{8,25},{9,... | collective-permute-start | bytes 6152 | tf_op jit(solution)/shard_map/ppermute | solution.py:555
  82.7 1.9 %collective-permute-start.36 = (f32[4,64,128]{2,1,0:T(8,128)S(1)}, f32[4,64,128]{2,1,0:T(8,128)S(1)}, u32[]{:S(2)}, u32[]{:S(2)}) collective-permute-start(f32[4,64,128]{2,1,0:T(8,128)S(1)} %wave_halo.29.cur.prev), channel_id=1, source_target_pairs={{0,4},{1,3},{2,6},{3,1},{4,0},{5,9},{6,2},{7,11},{8,12},{9,5},{10,... | collective-permute-start | bytes 393224 | tf_op jit(solution)/shard_map/ppermute | solution.py:551
  85.0 1.9 %gravity_adjoint.2.start_at = f32[8,16,128]{2,1,0:T(8,128)S(1)} custom-call(s32[513]{0:T(1024)S(1)} %pad_add_fusion.head, f32[4,128]{1,0:T(4,128)S(1)} %get-tuple-element.204.weights, f32[9088,128]{1,0:T(8,128)S(1)} %gravity_table.1.table, f32[8,16,128]{2,1,0:T(8,128)S(1)} %broadcast_in_dim.12.start_at), custom_call_target="tpu_custom_call" | custom-call | flops 8388608 | bytes 131072 | tf_op jit(solution)/shard_map/gravity_adjoint/pallas_call | solution.py:431
  88.5 2.5 %collective-permute-start.38 = (f32[4,64,128]{2,1,0:T(8,128)S(1)}, f32[4,64,128]{2,1,0:T(8,128)S(1)}, u32[]{:S(2)}, u32[]{:S(2)}) collective-permute-start(f32[4,64,128]{2,1,0:T(8,128)S(1)} %wave_halo.30.cur), channel_id=1, source_target_pairs={{0,4},{1,3},{2,6},{3,1},{4,0},{5,9},{6,2},{7,11},{8,12},{9,5},{10,... | collective-permute-start | bytes 393224 | tf_op jit(solution)/shard_map/ppermute | solution.py:551
  91.5 2.5 %gravity_adjoint.3 = f32[8,16,128]{2,1,0:T(8,128)} custom-call(s32[513]{0:T(1024)S(1)} %pad_add_fusion.head, f32[4,128]{1,0:T(4,128)S(1)} %get-tuple-element.204.weights, f32[9088,128]{1,0:T(8,128)S(1)} %gravity_table.1.table, f32[8,16,128]{2,1,0:T(8,128)S(1)} %gravity_adjoint.2.start_at), custom_call_target="tpu_custom_call" | custom-call | flops 8388608 | bytes 131072 | tf_op jit(solution)/shard_map/gravity_adjoint/pallas_call | solution.py:431
  96.3 1.7 %collective-permute-start.41 = (f32[32,128]{1,0:T(8,128)S(1)}, f32[32,128]{1,0:T(8,128)S(1)}, u32[]{:S(2)}, u32[]{:S(2)}) collective-permute-start(f32[32,128]{1,0:T(8,128)S(1)} %shard_map.133.first), channel_id=1, source_target_pairs={{0,5},{1,4},{2,7},{3,6},{4,1},{5,0},{6,3},{7,2},{8,13},{9,12},{10,... | collective-permute-start | bytes 49160 | tf_op jit(solution)/shard_map/ppermute | solution.py:555
  102.6 2.4 %collective-permute-start.44 = (f32[32,128]{1,0:T(8,128)S(1)}, f32[32,128]{1,0:T(8,128)S(1)}, u32[]{:S(2)}, u32[]{:S(2)}) collective-permute-start(f32[32,128]{1,0:T(8,128)S(1)} %shard_map.135.packed), channel_id=1, source_target_pairs={{0,17},{1,16},{2,19},{3,18},{4,21},{5,20},{6,23},{7,22},{8,25},{9,... | collective-permute-start | bytes 49160 | tf_op jit(solution)/shard_map/ppermute | solution.py:555
  105.0 1.7 %collective-permute-done.44.other = f32[32,128]{1,0:T(8,128)S(1)} collective-permute-done((f32[32,128]{1,0:T(8,128)S(1)}, f32[32,128]{1,0:T(8,128)S(1)}, u32[]{:S(2)}, u32[]{:S(2)}) %collective-permute-start.44) | collective-permute-done | bytes 16416 | tf_op jit(solution)/shard_map/ppermute | solution.py:555
  (125 shorter events, 37.0 us)
Async XLA Ops:
  1.5 6.7 %collective-permute-start = (f32[4,64,128]{2,1,0:T(8,128)S(1)}, f32[4,64,128]{2,1,0:T(8,128)S(1)}, u32[]{:S(2)}, u32[]{:S(2)}) collective-permute-start(f32[4,64,128]{2,1,0:T(8,128)S(1)} %first_planes.1.cur.prev), channel_id=1, source_target_pairs={{0,4},{1,3},{2,6},{3,1},{4,0},{5,9},{6,2},{7,11},{8,12},{9,5},{10,... | collective-permute-start | bytes 393224 | tf_op jit(solution)/shard_map/ppermute | solution.py:551
  4.5 3.7 %collective-permute-start.1 = (f32[4,64,128]{2,1,0:T(8,128)S(1)}, f32[4,64,128]{2,1,0:T(8,128)S(1)}, u32[]{:S(2)}, u32[]{:S(2)}) collective-permute-start(f32[4,64,128]{2,1,0:T(8,128)S(1)} %first_planes.1.cur.prev), channel_id=1, source_target_pairs={{0,1},{1,0},{2,3},{3,2},{4,5},{5,4},{6,7},{7,6},{8,9},{9,8},{10,11... | collective-permute-start | bytes 393224 | tf_op jit(solution)/shard_map/ppermute | solution.py:555
  8.3 5.5 %collective-permute-start.2 = (f32[4,64,128]{2,1,0:T(8,128)S(1)}, f32[4,64,128]{2,1,0:T(8,128)S(1)}, u32[]{:S(2)}, u32[]{:S(2)}) collective-permute-start(f32[4,64,128]{2,1,0:T(8,128)S(1)} %wave_halo.16.cur.prev), channel_id=1, source_target_pairs={{0,4},{1,3},{2,6},{3,1},{4,0},{5,9},{6,2},{7,11},{8,12},{9,5},{10,... | collective-permute-start | bytes 393224 | tf_op jit(solution)/shard_map/ppermute | solution.py:551
  10.8 3.0 %collective-permute-start.3 = (f32[4,64,128]{2,1,0:T(8,128)S(1)}, f32[4,64,128]{2,1,0:T(8,128)S(1)}, u32[]{:S(2)}, u32[]{:S(2)}) collective-permute-start(f32[4,64,128]{2,1,0:T(8,128)S(1)} %wave_halo.16.cur.prev), channel_id=1, source_target_pairs={{0,1},{1,0},{2,3},{3,2},{4,5},{5,4},{6,7},{7,6},{8,9},{9,8},{10,11... | collective-permute-start | bytes 393224 | tf_op jit(solution)/shard_map/ppermute | solution.py:555
  11.2 5.1 %collective-permute-start.4 = (f32[2,64,128]{2,1,0:T(8,128)S(1)}, f32[2,64,128]{2,1,0:T(8,128)S(1)}, u32[]{:S(2)}, u32[]{:S(2)}) collective-permute-start(f32[2,64,128]{2,1,0:T(8,128)S(1)} %get-tuple-element.123), channel_id=1, source_target_pairs={{0,4},{1,3},{2,6},{3,1},{4,0},{5,9},{6,2},{7,11},{8,12},{9,5},{10,... | collective-permute-start | bytes 196616 | tf_op jit(solution)/shard_map/ppermute | solution.py:551
  11.4 5.0 %collective-permute-start.5 = (f32[2,1,128]{2,1,0:T(1,128)S(1)}, f32[2,1,128]{2,1,0:T(1,128)S(1)}, u32[]{:S(2)}, u32[]{:S(2)}) collective-permute-start(f32[2,1,128]{2,1,0:T(1,128)S(1)} %get-tuple-element.125), channel_id=1, source_target_pairs={{0,1},{1,0},{2,3},{3,2},{4,5},{5,4},{6,7},{7,6},{8,9},{9,8},{10,11... | collective-permute-start | bytes 3080 | tf_op jit(solution)/shard_map/ppermute | solution.py:555
  13.8 5.0 %collective-permute-start.6 = (f32[4,64,128]{2,1,0:T(8,128)S(1)}, f32[4,64,128]{2,1,0:T(8,128)S(1)}, u32[]{:S(2)}, u32[]{:S(2)}) collective-permute-start(f32[4,64,128]{2,1,0:T(8,128)S(1)} %wave_halo.17.cur.prev), channel_id=1, source_target_pairs={{0,4},{1,3},{2,6},{3,1},{4,0},{5,9},{6,2},{7,11},{8,12},{9,5},{10,... | collective-permute-start | bytes 393224 | tf_op jit(solution)/shard_map/ppermute | solution.py:551
  16.4 5.2 %collective-permute-start.8 = (f32[2,2,128]{2,1,0:T(2,128)S(1)}, f32[2,2,128]{2,1,0:T(2,128)S(1)}, u32[]{:S(2)}, u32[]{:S(2)}) collective-permute-start(f32[2,2,128]{2,1,0:T(2,128)S(1)} %pad_maximum_fusion.1), channel_id=1, source_target_pairs={{0,2},{1,3},{2,0},{3,1},{4,6},{5,7},{6,4},{7,5},{8,10},{9,11},{10,... | collective-permute-start | bytes 6152 | tf_op jit(solution)/shard_map/ppermute | solution.py:555
  18.9 4.6 %collective-permute-start.10 = (f32[4,64,128]{2,1,0:T(8,128)S(1)}, f32[4,64,128]{2,1,0:T(8,128)S(1)}, u32[]{:S(2)}, u32[]{:S(2)}) collective-permute-start(f32[4,64,128]{2,1,0:T(8,128)S(1)} %wave_halo.18.cur.prev), channel_id=1, source_target_pairs={{0,1},{1,0},{2,3},{3,2},{4,5},{5,4},{6,7},{7,6},{8,9},{9,8},{10,11... | collective-permute-start | bytes 393224 | tf_op jit(solution)/shard_map/ppermute | solution.py:555
  19.0 6.1 %collective-permute-start.9 = (f32[4,64,128]{2,1,0:T(8,128)S(1)}, f32[4,64,128]{2,1,0:T(8,128)S(1)}, u32[]{:S(2)}, u32[]{:S(2)}) collective-permute-start(f32[4,64,128]{2,1,0:T(8,128)S(1)} %wave_halo.18.cur.prev), channel_id=1, source_target_pairs={{0,4},{1,3},{2,6},{3,1},{4,0},{5,9},{6,2},{7,11},{8,12},{9,5},{10,... | collective-permute-start | bytes 393224 | tf_op jit(solution)/shard_map/ppermute | solution.py:551
  25.2 5.5 %collective-permute-start.11 = (f32[4,64,128]{2,1,0:T(8,128)S(1)}, f32[4,64,128]{2,1,0:T(8,128)S(1)}, u32[]{:S(2)}, u32[]{:S(2)}) collective-permute-start(f32[4,64,128]{2,1,0:T(8,128)S(1)} %wave_halo.19.cur.prev), channel_id=1, source_target_pairs={{0,4},{1,3},{2,6},{3,1},{4,0},{5,9},{6,2},{7,11},{8,12},{9,5},{10,... | collective-permute-start | bytes 393224 | tf_op jit(solution)/shard_map/ppermute | solution.py:551
  30.7 5.2 %collective-permute-start.13 = (f32[4,64,128]{2,1,0:T(8,128)S(1)}, f32[4,64,128]{2,1,0:T(8,128)S(1)}, u32[]{:S(2)}, u32[]{:S(2)}) collective-permute-start(f32[4,64,128]{2,1,0:T(8,128)S(1)} %wave_halo.20.cur.prev), channel_id=1, source_target_pairs={{0,4},{1,3},{2,6},{3,1},{4,0},{5,9},{6,2},{7,11},{8,12},{9,5},{10,... | collective-permute-start | bytes 393224 | tf_op jit(solution)/shard_map/ppermute | solution.py:551
  36.0 5.0 %collective-permute-start.15 = (f32[4,64,128]{2,1,0:T(8,128)S(1)}, f32[4,64,128]{2,1,0:T(8,128)S(1)}, u32[]{:S(2)}, u32[]{:S(2)}) collective-permute-start(f32[4,64,128]{2,1,0:T(8,128)S(1)} %wave_halo.21.cur.prev), channel_id=1, source_target_pairs={{0,4},{1,3},{2,6},{3,1},{4,0},{5,9},{6,2},{7,11},{8,12},{9,5},{10,... | collective-permute-start | bytes 393224 | tf_op jit(solution)/shard_map/ppermute | solution.py:551
  41.1 5.0 %collective-permute-start.17 = (f32[4,64,128]{2,1,0:T(8,128)S(1)}, f32[4,64,128]{2,1,0:T(8,128)S(1)}, u32[]{:S(2)}, u32[]{:S(2)}) collective-permute-start(f32[4,64,128]{2,1,0:T(8,128)S(1)} %wave_halo.22.cur.prev), channel_id=1, source_target_pairs={{0,4},{1,3},{2,6},{3,1},{4,0},{5,9},{6,2},{7,11},{8,12},{9,5},{10,... | collective-permute-start | bytes 393224 | tf_op jit(solution)/shard_map/ppermute | solution.py:551
  46.2 5.0 %collective-permute-start.19 = (f32[4,64,128]{2,1,0:T(8,128)S(1)}, f32[4,64,128]{2,1,0:T(8,128)S(1)}, u32[]{:S(2)}, u32[]{:S(2)}) collective-permute-start(f32[4,64,128]{2,1,0:T(8,128)S(1)} %wave_halo.23.cur.prev), channel_id=1, source_target_pairs={{0,4},{1,3},{2,6},{3,1},{4,0},{5,9},{6,2},{7,11},{8,12},{9,5},{10,... | collective-permute-start | bytes 393224 | tf_op jit(solution)/shard_map/ppermute | solution.py:551
  51.3 5.0 %collective-permute-start.22 = (f32[4,64,128]{2,1,0:T(8,128)S(1)}, f32[4,64,128]{2,1,0:T(8,128)S(1)}, u32[]{:S(2)}, u32[]{:S(2)}) collective-permute-start(f32[4,64,128]{2,1,0:T(8,128)S(1)} %wave_halo.24.cur.prev), channel_id=1, source_target_pairs={{0,4},{1,3},{2,6},{3,1},{4,0},{5,9},{6,2},{7,11},{8,12},{9,5},{10,... | collective-permute-start | bytes 393224 | tf_op jit(solution)/shard_map/ppermute | solution.py:551
  56.4 5.0 %collective-permute-start.24 = (f32[4,64,128]{2,1,0:T(8,128)S(1)}, f32[4,64,128]{2,1,0:T(8,128)S(1)}, u32[]{:S(2)}, u32[]{:S(2)}) collective-permute-start(f32[4,64,128]{2,1,0:T(8,128)S(1)} %wave_halo.25.cur.prev), channel_id=1, source_target_pairs={{0,4},{1,3},{2,6},{3,1},{4,0},{5,9},{6,2},{7,11},{8,12},{9,5},{10,... | collective-permute-start | bytes 393224 | tf_op jit(solution)/shard_map/ppermute | solution.py:551
  61.5 5.3 %collective-permute-start.27 = (f32[4,64,128]{2,1,0:T(8,128)S(1)}, f32[4,64,128]{2,1,0:T(8,128)S(1)}, u32[]{:S(2)}, u32[]{:S(2)}) collective-permute-start(f32[4,64,128]{2,1,0:T(8,128)S(1)} %wave_halo.26.cur.prev), channel_id=1, source_target_pairs={{0,4},{1,3},{2,6},{3,1},{4,0},{5,9},{6,2},{7,11},{8,12},{9,5},{10,... | collective-permute-start | bytes 393224 | tf_op jit(solution)/shard_map/ppermute | solution.py:551
  66.9 5.5 %collective-permute-start.30 = (f32[4,64,128]{2,1,0:T(8,128)S(1)}, f32[4,64,128]{2,1,0:T(8,128)S(1)}, u32[]{:S(2)}, u32[]{:S(2)}) collective-permute-start(f32[4,64,128]{2,1,0:T(8,128)S(1)} %wave_halo.27.cur.prev), channel_id=1, source_target_pairs={{0,4},{1,3},{2,6},{3,1},{4,0},{5,9},{6,2},{7,11},{8,12},{9,5},{10,... | collective-permute-start | bytes 393224 | tf_op jit(solution)/shard_map/ppermute | solution.py:551
  69.0 3.4 %collective-permute-start.31 = (f32[4,64,128]{2,1,0:T(8,128)S(1)}, f32[4,64,128]{2,1,0:T(8,128)S(1)}, u32[]{:S(2)}, u32[]{:S(2)}) collective-permute-start(f32[4,64,128]{2,1,0:T(8,128)S(1)} %wave_halo.27.cur.prev), channel_id=1, source_target_pairs={{0,1},{1,0},{2,3},{3,2},{4,5},{5,4},{6,7},{7,6},{8,9},{9,8},{10,11... | collective-permute-start | bytes 393224 | tf_op jit(solution)/shard_map/ppermute | solution.py:555
  69.0 3.0 %collective-permute-start.29 = (f32[4,128]{1,0:T(4,128)S(1)}, f32[4,128]{1,0:T(4,128)S(1)}, u32[]{:S(2)}, u32[]{:S(2)}) collective-permute-start(f32[4,128]{1,0:T(4,128)S(1)} %shard_map.129.first), channel_id=1, source_target_pairs={{0,5},{1,4},{2,7},{3,6},{4,1},{5,0},{6,3},{7,2},{8,13},{9,12},{10,... | collective-permute-start | bytes 6152 | tf_op jit(solution)/shard_map/ppermute | solution.py:555
  72.5 10.1 %collective-permute-start.33 = (f32[4,64,128]{2,1,0:T(8,128)S(1)}, f32[4,64,128]{2,1,0:T(8,128)S(1)}, u32[]{:S(2)}, u32[]{:S(2)}) collective-permute-start(f32[4,64,128]{2,1,0:T(8,128)S(1)} %wave_halo.28.cur.prev), channel_id=1, source_target_pairs={{0,4},{1,3},{2,6},{3,1},{4,0},{5,9},{6,2},{7,11},{8,12},{9,5},{10,... | collective-permute-start | bytes 393224 | tf_op jit(solution)/shard_map/ppermute | solution.py:551
  74.1 8.5 %collective-permute-start.34 = (f32[4,64,128]{2,1,0:T(8,128)S(1)}, f32[4,64,128]{2,1,0:T(8,128)S(1)}, u32[]{:S(2)}, u32[]{:S(2)}) collective-permute-start(f32[4,64,128]{2,1,0:T(8,128)S(1)} %wave_halo.28.cur.prev), channel_id=1, source_target_pairs={{0,1},{1,0},{2,3},{3,2},{4,5},{5,4},{6,7},{7,6},{8,9},{9,8},{10,11... | collective-permute-start | bytes 393224 | tf_op jit(solution)/shard_map/ppermute | solution.py:555
  74.3 3.9 %collective-permute-start.32 = (f32[4,128]{1,0:T(4,128)S(1)}, f32[4,128]{1,0:T(4,128)S(1)}, u32[]{:S(2)}, u32[]{:S(2)}) collective-permute-start(f32[4,128]{1,0:T(4,128)S(1)} %shard_map.130.first), channel_id=1, source_target_pairs={{0,9},{1,8},{2,11},{3,10},{4,13},{5,12},{6,15},{7,14},{8,1},{9,0},... | collective-permute-start | bytes 6152 | tf_op jit(solution)/shard_map/ppermute | solution.py:555
  78.2 3.9 %collective-permute-start.35 = (f32[4,128]{1,0:T(4,128)S(1)}, f32[4,128]{1,0:T(4,128)S(1)}, u32[]{:S(2)}, u32[]{:S(2)}) collective-permute-start(f32[4,128]{1,0:T(4,128)S(1)} %shard_map.131.packed), channel_id=1, source_target_pairs={{0,17},{1,16},{2,19},{3,18},{4,21},{5,20},{6,23},{7,22},{8,25},{9,... | collective-permute-start | bytes 6152 | tf_op jit(solution)/shard_map/ppermute | solution.py:555
  82.7 5.8 %collective-permute-start.36 = (f32[4,64,128]{2,1,0:T(8,128)S(1)}, f32[4,64,128]{2,1,0:T(8,128)S(1)}, u32[]{:S(2)}, u32[]{:S(2)}) collective-permute-start(f32[4,64,128]{2,1,0:T(8,128)S(1)} %wave_halo.29.cur.prev), channel_id=1, source_target_pairs={{0,4},{1,3},{2,6},{3,1},{4,0},{5,9},{6,2},{7,11},{8,12},{9,5},{10,... | collective-permute-start | bytes 393224 | tf_op jit(solution)/shard_map/ppermute | solution.py:551
  84.6 3.9 %collective-permute-start.37 = (f32[4,64,128]{2,1,0:T(8,128)S(1)}, f32[4,64,128]{2,1,0:T(8,128)S(1)}, u32[]{:S(2)}, u32[]{:S(2)}) collective-permute-start(f32[4,64,128]{2,1,0:T(8,128)S(1)} %wave_halo.29.cur.prev), channel_id=1, source_target_pairs={{0,1},{1,0},{2,3},{3,2},{4,5},{5,4},{6,7},{7,6},{8,9},{9,8},{10,11... | collective-permute-start | bytes 393224 | tf_op jit(solution)/shard_map/ppermute | solution.py:555
  88.5 5.5 %collective-permute-start.38 = (f32[4,64,128]{2,1,0:T(8,128)S(1)}, f32[4,64,128]{2,1,0:T(8,128)S(1)}, u32[]{:S(2)}, u32[]{:S(2)}) collective-permute-start(f32[4,64,128]{2,1,0:T(8,128)S(1)} %wave_halo.30.cur), channel_id=1, source_target_pairs={{0,4},{1,3},{2,6},{3,1},{4,0},{5,9},{6,2},{7,11},{8,12},{9,5},{10,... | collective-permute-start | bytes 393224 | tf_op jit(solution)/shard_map/ppermute | solution.py:551
  94.1 6.6 %collective-permute-start.43 = (f32[4,64,128]{2,1,0:T(8,128)S(1)}, f32[4,64,128]{2,1,0:T(8,128)S(1)}, u32[]{:S(2)}, u32[]{:S(2)}) collective-permute-start(f32[4,64,128]{2,1,0:T(8,128)S(1)} %wave_halo.31.cur.own), channel_id=1, source_target_pairs={{0,1},{1,0},{2,3},{3,2},{4,5},{5,4},{6,7},{7,6},{8,9},{9,8},{10,11... | collective-permute-start | bytes 393224 | tf_op jit(solution)/shard_map/ppermute | solution.py:555
  96.3 3.2 %collective-permute-start.41 = (f32[32,128]{1,0:T(8,128)S(1)}, f32[32,128]{1,0:T(8,128)S(1)}, u32[]{:S(2)}, u32[]{:S(2)}) collective-permute-start(f32[32,128]{1,0:T(8,128)S(1)} %shard_map.133.first), channel_id=1, source_target_pairs={{0,5},{1,4},{2,7},{3,6},{4,1},{5,0},{6,3},{7,2},{8,13},{9,12},{10,... | collective-permute-start | bytes 49160 | tf_op jit(solution)/shard_map/ppermute | solution.py:555
  99.4 3.2 %collective-permute-start.42 = (f32[32,128]{1,0:T(8,128)S(1)}, f32[32,128]{1,0:T(8,128)S(1)}, u32[]{:S(2)}, u32[]{:S(2)}) collective-permute-start(f32[32,128]{1,0:T(8,128)S(1)} %shard_map.134.first), channel_id=1, source_target_pairs={{0,9},{1,8},{2,11},{3,10},{4,13},{5,12},{6,15},{7,14},{8,1},{9,0},... | collective-permute-start | bytes 49160 | tf_op jit(solution)/shard_map/ppermute | solution.py:555
  102.6 4.1 %collective-permute-start.44 = (f32[32,128]{1,0:T(8,128)S(1)}, f32[32,128]{1,0:T(8,128)S(1)}, u32[]{:S(2)}, u32[]{:S(2)}) collective-permute-start(f32[32,128]{1,0:T(8,128)S(1)} %shard_map.135.packed), channel_id=1, source_target_pairs={{0,17},{1,16},{2,19},{3,18},{4,21},{5,20},{6,23},{7,22},{8,25},{9,... | collective-permute-start | bytes 49160 | tf_op jit(solution)/shard_map/ppermute | solution.py:555
  (16 other events, 69.5 us)
where the time goes:
time: 107 us
  starting transfers between devices  50.8 us (47%)
  Pallas kernels  28.6 us (27%)
  waiting for transfers between devices  26.1 us (24%)
  between operations  1.72 us (2%)
    ppermute x17, starting transfers between devices, across(): return lax.ppermute(value, AXES, chain)  35.8 us
    ppermute x28, starting transfers between devices, swap(): return lax.ppermute(value, AXES, pairs)  15 us
    ppermute x17, waiting for transfers between devices, across(): return lax.ppermute(value, AXES, chain)  13.2 us
    ppermute x28, waiting for transfers between devices, swap(): return lax.ppermute(value, AXES, pairs)  12.9 us
    pallas_call x5, Pallas kernels, gravity_forward(): pl.pallas_call(functools.partial(forward_kernel, first, guard, total_x, l...  9.5 us
    pallas_call x16, Pallas kernels, local_step(): pl.pallas_call(functools.partial(local_kernel, step), out_shape=(shape(cu...  6.11 us
    pallas_call x2, Pallas kernels, gravity_adjoint(): pl.pallas_call(functools.partial(adjoint_kernel, lines, guard, total_x, l...  4.44 us
  transfers between devices with their start and end apart: 45, of which 22 were waited for; matrix products, arithmetic and copies ran while one was open for 0% of the time, Pallas kernels for 24%

commit v1 on v0

--- a/solution.py
+++ b/solution.py
@@ -694,8 +694,10 @@
     jobs = [exchange(1 << b) for b in range(stations.bit_length() - 1)]
     if hidden:
         jobs += [build_table] + [forward(i) for i in range(pieces)] + [both(predict, cross)]
-        jobs += [add_up(1 << b) for b in range(count.bit_length() - 1)] + [residual]
-        jobs += [adjoint(range(lines // 2)), adjoint(range(lines // 2, lines))]
+        jobs += [add_up(1 << b) for b in range(count.bit_length() - 1)]
+        quarter = lines // 4
+        jobs += [both(residual, adjoint(range(quarter)))]
+        jobs += [adjoint(range(quarter, 3 * quarter)), adjoint(range(3 * quarter, lines))]
     jobs[0] = both(send_edges, jobs[0])
     jobs[1] = both(share_edges, jobs[1])
     if not hidden:

time: 107 us -> 109 us (1.019)
    pallas_call x2 -> x3, Pallas kernels: 4.44 us -> 5.05 us  [gravity_adjoint(): pl.pallas_call(functools.partial(adjoint_kernel, lines, guard, total_x, l...]
  transfers between devices with their start and end apart: 45 -> 45, of which waited for: 22 -> 23; matrix products, arithmetic and copies ran while one was open for 0% -> 0% of each run, Pallas kernels for 24% -> 25%
where the time goes in v1:
time: 109 us
  starting transfers between devices  51.1 us (47%)
  Pallas kernels  29.2 us (27%)
  waiting for transfers between devices  26.4 us (24%)
  between operations  1.75 us (2%)
    ppermute x17, starting transfers between devices, across(): return lax.ppermute(value, AXES, chain)  35.8 us
    ppermute x28, starting transfers between devices, swap(): return lax.ppermute(value, AXES, pairs)  15.3 us
    ppermute x17, waiting for transfers between devices, across(): return lax.ppermute(value, AXES, chain)  13.9 us
    ppermute x28, waiting for transfers between devices, swap(): return lax.ppermute(value, AXES, pairs)  12.5 us
    pallas_call x5, Pallas kernels, gravity_forward(): pl.pallas_call(functools.partial(forward_kernel, first, guard, total_x, l...  9.5 us
    pallas_call x16, Pallas kernels, local_step(): pl.pallas_call(functools.partial(local_kernel, step), out_shape=(shape(cu...  6.12 us
    pallas_call x3, Pallas kernels, gravity_adjoint(): pl.pallas_call(functools.partial(adjoint_kernel, lines, guard, total_x, l...  5.05 us
  transfers between devices with their start and end apart: 45, of which 23 were waited for; matrix products, arithmetic and copies ran while one was open for 0% of the time, Pallas kernels for 25%

profile of v1, /device:TPU:0, one launch (start us, length us, event | category | flops | bytes accessed | tf_op | source)
XLA Modules:
  0.0 108.5 jit_solution(3904302112380155089)
XLA Ops:
  1.5 3.0 %collective-permute-start = (f32[4,64,128]{2,1,0:T(8,128)S(1)}, f32[4,64,128]{2,1,0:T(8,128)S(1)}, u32[]{:S(2)}, u32[]{:S(2)}) collective-permute-start(f32[4,64,128]{2,1,0:T(8,128)S(1)} %first_planes.1.cur.prev), channel_id=1, source_target_pairs={{0,4},{1,3},{2,6},{3,1},{4,0},{5,9},{6,2},{7,11},{8,12},{9,5},{10,... | collective-permute-start | bytes 393224 | tf_op jit(solution)/shard_map/ppermute | solution.py:551
  8.3 2.5 %collective-permute-start.2 = (f32[4,64,128]{2,1,0:T(8,128)S(1)}, f32[4,64,128]{2,1,0:T(8,128)S(1)}, u32[]{:S(2)}, u32[]{:S(2)}) collective-permute-start(f32[4,64,128]{2,1,0:T(8,128)S(1)} %wave_halo.16.cur.prev), channel_id=1, source_target_pairs={{0,4},{1,3},{2,6},{3,1},{4,0},{5,9},{6,2},{7,11},{8,12},{9,5},{10,... | collective-permute-start | bytes 393224 | tf_op jit(solution)/shard_map/ppermute | solution.py:551
  11.4 1.7 %collective-permute-start.5 = (f32[2,1,128]{2,1,0:T(1,128)S(1)}, f32[2,1,128]{2,1,0:T(1,128)S(1)}, u32[]{:S(2)}, u32[]{:S(2)}) collective-permute-start(f32[2,1,128]{2,1,0:T(1,128)S(1)} %get-tuple-element.127), channel_id=1, source_target_pairs={{0,1},{1,0},{2,3},{3,2},{4,5},{5,4},{6,7},{7,6},{8,9},{9,8},{10,11... | collective-permute-start | bytes 3080 | tf_op jit(solution)/shard_map/ppermute | solution.py:555
  13.8 2.1 %collective-permute-start.6 = (f32[4,64,128]{2,1,0:T(8,128)S(1)}, f32[4,64,128]{2,1,0:T(8,128)S(1)}, u32[]{:S(2)}, u32[]{:S(2)}) collective-permute-start(f32[4,64,128]{2,1,0:T(8,128)S(1)} %wave_halo.17.cur.prev), channel_id=1, source_target_pairs={{0,4},{1,3},{2,6},{3,1},{4,0},{5,9},{6,2},{7,11},{8,12},{9,5},{10,... | collective-permute-start | bytes 393224 | tf_op jit(solution)/shard_map/ppermute | solution.py:551
  19.0 2.2 %collective-permute-start.9 = (f32[4,64,128]{2,1,0:T(8,128)S(1)}, f32[4,64,128]{2,1,0:T(8,128)S(1)}, u32[]{:S(2)}, u32[]{:S(2)}) collective-permute-start(f32[4,64,128]{2,1,0:T(8,128)S(1)} %wave_halo.18.cur.prev), channel_id=1, source_target_pairs={{0,4},{1,3},{2,6},{3,1},{4,0},{5,9},{6,2},{7,11},{8,12},{9,5},{10,... | collective-permute-start | bytes 393224 | tf_op jit(solution)/shard_map/ppermute | solution.py:551
  21.7 1.8 %gravity_table.1.table = f32[9088,128]{1,0:T(8,128)S(1)} custom-call(s32[1]{0:T(128)} %constant.54.clone.1.head), custom_call_target="tpu_custom_call" | custom-call | flops 23265280 | bytes 4653056 | tf_op jit(solution)/shard_map/gravity_table/pallas_call | solution.py:346
  25.2 2.5 %collective-permute-start.11 = (f32[4,64,128]{2,1,0:T(8,128)S(1)}, f32[4,64,128]{2,1,0:T(8,128)S(1)}, u32[]{:S(2)}, u32[]{:S(2)}) collective-permute-start(f32[4,64,128]{2,1,0:T(8,128)S(1)} %wave_halo.19.cur.prev), channel_id=1, source_target_pairs={{0,4},{1,3},{2,6},{3,1},{4,0},{5,9},{6,2},{7,11},{8,12},{9,5},{10,... | collective-permute-start | bytes 393224 | tf_op jit(solution)/shard_map/ppermute | solution.py:551
  28.1 1.9 %gravity_forward.5.refs_0_ = f32[104,128]{1,0:T(8,128)S(1)} custom-call(s32[513]{0:T(1024)S(1)} %pad_add_fusion.head, f32[9088,128]{1,0:T(8,128)S(1)} %gravity_table.1.table, f32[4,64,128]{2,1,0:T(8,128)S(1)} %get-tuple-element.143.dens), custom_call_target="tpu_custom_call" | custom-call | flops 13631488 | bytes 131072 | tf_op jit(solution)/shard_map/gravity_forward/pallas_call | solution.py:391
  30.7 2.3 %collective-permute-start.13 = (f32[4,64,128]{2,1,0:T(8,128)S(1)}, f32[4,64,128]{2,1,0:T(8,128)S(1)}, u32[]{:S(2)}, u32[]{:S(2)}) collective-permute-start(f32[4,64,128]{2,1,0:T(8,128)S(1)} %wave_halo.20.cur.prev), channel_id=1, source_target_pairs={{0,4},{1,3},{2,6},{3,1},{4,0},{5,9},{6,2},{7,11},{8,12},{9,5},{10,... | collective-permute-start | bytes 393224 | tf_op jit(solution)/shard_map/ppermute | solution.py:551
  33.4 1.9 %gravity_forward.6.refs_1_ = f32[104,128]{1,0:T(8,128)S(1)} custom-call(s32[513]{0:T(1024)S(1)} %pad_add_fusion.head, f32[9088,128]{1,0:T(8,128)S(1)} %gravity_table.1.table, f32[4,64,128]{2,1,0:T(8,128)S(1)} %get-tuple-element.143.dens), custom_call_target="tpu_custom_call" | custom-call | flops 13631488 | bytes 131072 | tf_op jit(solution)/shard_map/gravity_forward/pallas_call | solution.py:391
  36.0 2.1 %collective-permute-start.15 = (f32[4,64,128]{2,1,0:T(8,128)S(1)}, f32[4,64,128]{2,1,0:T(8,128)S(1)}, u32[]{:S(2)}, u32[]{:S(2)}) collective-permute-start(f32[4,64,128]{2,1,0:T(8,128)S(1)} %wave_halo.21.cur.prev), channel_id=1, source_target_pairs={{0,4},{1,3},{2,6},{3,1},{4,0},{5,9},{6,2},{7,11},{8,12},{9,5},{10,... | collective-permute-start | bytes 393224 | tf_op jit(solution)/shard_map/ppermute | solution.py:551
  38.5 1.9 %gravity_forward.7.refs_2_ = f32[104,128]{1,0:T(8,128)S(1)} custom-call(s32[513]{0:T(1024)S(1)} %pad_add_fusion.head, f32[9088,128]{1,0:T(8,128)S(1)} %gravity_table.1.table, f32[4,64,128]{2,1,0:T(8,128)S(1)} %get-tuple-element.143.dens), custom_call_target="tpu_custom_call" | custom-call | flops 13631488 | bytes 131072 | tf_op jit(solution)/shard_map/gravity_forward/pallas_call | solution.py:391
  41.1 2.1 %collective-permute-start.17 = (f32[4,64,128]{2,1,0:T(8,128)S(1)}, f32[4,64,128]{2,1,0:T(8,128)S(1)}, u32[]{:S(2)}, u32[]{:S(2)}) collective-permute-start(f32[4,64,128]{2,1,0:T(8,128)S(1)} %wave_halo.22.cur.prev), channel_id=1, source_target_pairs={{0,4},{1,3},{2,6},{3,1},{4,0},{5,9},{6,2},{7,11},{8,12},{9,5},{10,... | collective-permute-start | bytes 393224 | tf_op jit(solution)/shard_map/ppermute | solution.py:551
  43.6 1.9 %gravity_forward.8.refs_3_ = f32[104,128]{1,0:T(8,128)S(1)} custom-call(s32[513]{0:T(1024)S(1)} %pad_add_fusion.head, f32[9088,128]{1,0:T(8,128)S(1)} %gravity_table.1.table, f32[4,64,128]{2,1,0:T(8,128)S(1)} %get-tuple-element.143.dens), custom_call_target="tpu_custom_call" | custom-call | flops 13631488 | bytes 131072 | tf_op jit(solution)/shard_map/gravity_forward/pallas_call | solution.py:391
  46.2 2.1 %collective-permute-start.19 = (f32[4,64,128]{2,1,0:T(8,128)S(1)}, f32[4,64,128]{2,1,0:T(8,128)S(1)}, u32[]{:S(2)}, u32[]{:S(2)}) collective-permute-start(f32[4,64,128]{2,1,0:T(8,128)S(1)} %wave_halo.23.cur.prev), channel_id=1, source_target_pairs={{0,4},{1,3},{2,6},{3,1},{4,0},{5,9},{6,2},{7,11},{8,12},{9,5},{10,... | collective-permute-start | bytes 393224 | tf_op jit(solution)/shard_map/ppermute | solution.py:551
  48.7 1.8 %gravity_forward.9.refs_4_ = f32[96,128]{1,0:T(8,128)S(1)} custom-call(s32[513]{0:T(1024)S(1)} %pad_add_fusion.head, f32[9088,128]{1,0:T(8,128)S(1)} %gravity_table.1.table, f32[4,64,128]{2,1,0:T(8,128)S(1)} %get-tuple-element.143.dens), custom_call_target="tpu_custom_call" | custom-call | flops 12582912 | bytes 131072 | tf_op jit(solution)/shard_map/gravity_forward/pallas_call | solution.py:391
  51.3 2.1 %collective-permute-start.22 = (f32[4,64,128]{2,1,0:T(8,128)S(1)}, f32[4,64,128]{2,1,0:T(8,128)S(1)}, u32[]{:S(2)}, u32[]{:S(2)}) collective-permute-start(f32[4,64,128]{2,1,0:T(8,128)S(1)} %wave_halo.24.cur.prev), channel_id=1, source_target_pairs={{0,4},{1,3},{2,6},{3,1},{4,0},{5,9},{6,2},{7,11},{8,12},{9,5},{10,... | collective-permute-start | bytes 393224 | tf_op jit(solution)/shard_map/ppermute | solution.py:551
  56.4 2.1 %collective-permute-start.24 = (f32[4,64,128]{2,1,0:T(8,128)S(1)}, f32[4,64,128]{2,1,0:T(8,128)S(1)}, u32[]{:S(2)}, u32[]{:S(2)}) collective-permute-start(f32[4,64,128]{2,1,0:T(8,128)S(1)} %wave_halo.25.cur.prev), channel_id=1, source_target_pairs={{0,4},{1,3},{2,6},{3,1},{4,0},{5,9},{6,2},{7,11},{8,12},{9,5},{10,... | collective-permute-start | bytes 393224 | tf_op jit(solution)/shard_map/ppermute | solution.py:551
  59.1 2.4 %collective-permute-done.24.outer = f32[4,64,128]{2,1,0:T(8,128)S(1)} collective-permute-done((f32[4,64,128]{2,1,0:T(8,128)S(1)}, f32[4,64,128]{2,1,0:T(8,128)S(1)}, u32[]{:S(2)}, u32[]{:S(2)}) %collective-permute-start.24) | collective-permute-done | bytes 131104 | tf_op jit(solution)/shard_map/ppermute | solution.py:551
  61.5 2.3 %collective-permute-start.27 = (f32[4,64,128]{2,1,0:T(8,128)S(1)}, f32[4,64,128]{2,1,0:T(8,128)S(1)}, u32[]{:S(2)}, u32[]{:S(2)}) collective-permute-start(f32[4,64,128]{2,1,0:T(8,128)S(1)} %wave_halo.26.cur.prev), channel_id=1, source_target_pairs={{0,4},{1,3},{2,6},{3,1},{4,0},{5,9},{6,2},{7,11},{8,12},{9,5},{10,... | collective-permute-start | bytes 393224 | tf_op jit(solution)/shard_map/ppermute | solution.py:551
  66.9 2.1 %collective-permute-start.30 = (f32[4,64,128]{2,1,0:T(8,128)S(1)}, f32[4,64,128]{2,1,0:T(8,128)S(1)}, u32[]{:S(2)}, u32[]{:S(2)}) collective-permute-start(f32[4,64,128]{2,1,0:T(8,128)S(1)} %wave_halo.27.cur.prev), channel_id=1, source_target_pairs={{0,4},{1,3},{2,6},{3,1},{4,0},{5,9},{6,2},{7,11},{8,12},{9,5},{10,... | collective-permute-start | bytes 393224 | tf_op jit(solution)/shard_map/ppermute | solution.py:551
  69.2 2.8 %collective-permute-done.29.second = f32[4,128]{1,0:T(4,128)S(1)} collective-permute-done((f32[4,128]{1,0:T(4,128)S(1)}, f32[4,128]{1,0:T(4,128)S(1)}, u32[]{:S(2)}, u32[]{:S(2)}) %collective-permute-start.29) | collective-permute-done | bytes 2080 | tf_op jit(solution)/shard_map/ppermute | solution.py:555
  74.3 1.9 %collective-permute-start.32 = (f32[4,128]{1,0:T(4,128)S(1)}, f32[4,128]{1,0:T(4,128)S(1)}, u32[]{:S(2)}, u32[]{:S(2)}) collective-permute-start(f32[4,128]{1,0:T(4,128)S(1)} %shard_map.130.first), channel_id=1, source_target_pairs={{0,9},{1,8},{2,11},{3,10},{4,13},{5,12},{6,15},{7,14},{8,1},{9,0},... | collective-permute-start | bytes 6152 | tf_op jit(solution)/shard_map/ppermute | solution.py:555
  76.2 2.0 %collective-permute-done.32.second = f32[4,128]{1,0:T(4,128)S(1)} collective-permute-done((f32[4,128]{1,0:T(4,128)S(1)}, f32[4,128]{1,0:T(4,128)S(1)}, u32[]{:S(2)}, u32[]{:S(2)}) %collective-permute-start.32) | collective-permute-done | bytes 2080 | tf_op jit(solution)/shard_map/ppermute | solution.py:555
  78.2 2.3 %collective-permute-start.33 = (f32[4,128]{1,0:T(4,128)S(1)}, f32[4,128]{1,0:T(4,128)S(1)}, u32[]{:S(2)}, u32[]{:S(2)}) collective-permute-start(f32[4,128]{1,0:T(4,128)S(1)} %shard_map.131.packed), channel_id=1, source_target_pairs={{0,17},{1,16},{2,19},{3,18},{4,21},{5,20},{6,23},{7,22},{8,25},{9,... | collective-permute-start | bytes 6152 | tf_op jit(solution)/shard_map/ppermute | solution.py:555
  84.0 1.9 %collective-permute-start.36 = (f32[4,64,128]{2,1,0:T(8,128)S(1)}, f32[4,64,128]{2,1,0:T(8,128)S(1)}, u32[]{:S(2)}, u32[]{:S(2)}) collective-permute-start(f32[4,64,128]{2,1,0:T(8,128)S(1)} %wave_halo.29.cur.prev), channel_id=1, source_target_pairs={{0,4},{1,3},{2,6},{3,1},{4,0},{5,9},{6,2},{7,11},{8,12},{9,5},{10,... | collective-permute-start | bytes 393224 | tf_op jit(solution)/shard_map/ppermute | solution.py:551
  86.3 1.9 %gravity_adjoint.4.start_at = f32[8,16,128]{2,1,0:T(8,128)S(1)} custom-call(s32[513]{0:T(1024)S(1)} %pad_add_fusion.head, f32[4,128]{1,0:T(4,128)S(1)} %get-tuple-element.208.weights, f32[9088,128]{1,0:T(8,128)S(1)} %gravity_table.1.table, f32[8,16,128]{2,1,0:T(8,128)S(1)} %gravity_adjoint.3.start_at), custom_call_target="tpu_custom_call" | custom-call | flops 8388608 | bytes 131072 | tf_op jit(solution)/shard_map/gravity_adjoint/pallas_call | solution.py:431
  89.8 2.5 %collective-permute-start.38 = (f32[4,64,128]{2,1,0:T(8,128)S(1)}, f32[4,64,128]{2,1,0:T(8,128)S(1)}, u32[]{:S(2)}, u32[]{:S(2)}) collective-permute-start(f32[4,64,128]{2,1,0:T(8,128)S(1)} %wave_halo.30.cur), channel_id=1, source_target_pairs={{0,4},{1,3},{2,6},{3,1},{4,0},{5,9},{6,2},{7,11},{8,12},{9,5},{10,... | collective-permute-start | bytes 393224 | tf_op jit(solution)/shard_map/ppermute | solution.py:551
  92.8 1.9 %gravity_adjoint.5 = f32[8,16,128]{2,1,0:T(8,128)} custom-call(s32[513]{0:T(1024)S(1)} %pad_add_fusion.head, f32[4,128]{1,0:T(4,128)S(1)} %get-tuple-element.208.weights, f32[9088,128]{1,0:T(8,128)S(1)} %gravity_table.1.table, f32[8,16,128]{2,1,0:T(8,128)S(1)} %gravity_adjoint.4.start_at), custom_call_target="tpu_custom_call" | custom-call | flops 4194304 | bytes 131072 | tf_op jit(solution)/shard_map/gravity_adjoint/pallas_call | solution.py:431
  97.2 2.0 %collective-permute-start.41 = (f32[32,128]{1,0:T(8,128)S(1)}, f32[32,128]{1,0:T(8,128)S(1)}, u32[]{:S(2)}, u32[]{:S(2)}) collective-permute-start(f32[32,128]{1,0:T(8,128)S(1)} %shard_map.133.first), channel_id=1, source_target_pairs={{0,5},{1,4},{2,7},{3,6},{4,1},{5,0},{6,3},{7,2},{8,13},{9,12},{10,... | collective-permute-start | bytes 49160 | tf_op jit(solution)/shard_map/ppermute | solution.py:555
  103.9 2.4 %collective-permute-start.44 = (f32[32,128]{1,0:T(8,128)S(1)}, f32[32,128]{1,0:T(8,128)S(1)}, u32[]{:S(2)}, u32[]{:S(2)}) collective-permute-start(f32[32,128]{1,0:T(8,128)S(1)} %shard_map.135.packed), channel_id=1, source_target_pairs={{0,17},{1,16},{2,19},{3,18},{4,21},{5,20},{6,23},{7,22},{8,25},{9,... | collective-permute-start | bytes 49160 | tf_op jit(solution)/shard_map/ppermute | solution.py:555
  106.2 1.7 %collective-permute-done.44.other = f32[32,128]{1,0:T(8,128)S(1)} collective-permute-done((f32[32,128]{1,0:T(8,128)S(1)}, f32[32,128]{1,0:T(8,128)S(1)}, u32[]{:S(2)}, u32[]{:S(2)}) %collective-permute-start.44) | collective-permute-done | bytes 16416 | tf_op jit(solution)/shard_map/ppermute | solution.py:555
  (126 shorter events, 38.6 us)
Async XLA Ops:
  1.5 6.7 %collective-permute-start = (f32[4,64,128]{2,1,0:T(8,128)S(1)}, f32[4,64,128]{2,1,0:T(8,128)S(1)}, u32[]{:S(2)}, u32[]{:S(2)}) collective-permute-start(f32[4,64,128]{2,1,0:T(8,128)S(1)} %first_planes.1.cur.prev), channel_id=1, source_target_pairs={{0,4},{1,3},{2,6},{3,1},{4,0},{5,9},{6,2},{7,11},{8,12},{9,5},{10,... | collective-permute-start | bytes 393224 | tf_op jit(solution)/shard_map/ppermute | solution.py:551
  4.5 3.7 %collective-permute-start.1 = (f32[4,64,128]{2,1,0:T(8,128)S(1)}, f32[4,64,128]{2,1,0:T(8,128)S(1)}, u32[]{:S(2)}, u32[]{:S(2)}) collective-permute-start(f32[4,64,128]{2,1,0:T(8,128)S(1)} %first_planes.1.cur.prev), channel_id=1, source_target_pairs={{0,1},{1,0},{2,3},{3,2},{4,5},{5,4},{6,7},{7,6},{8,9},{9,8},{10,11... | collective-permute-start | bytes 393224 | tf_op jit(solution)/shard_map/ppermute | solution.py:555
  8.3 5.5 %collective-permute-start.2 = (f32[4,64,128]{2,1,0:T(8,128)S(1)}, f32[4,64,128]{2,1,0:T(8,128)S(1)}, u32[]{:S(2)}, u32[]{:S(2)}) collective-permute-start(f32[4,64,128]{2,1,0:T(8,128)S(1)} %wave_halo.16.cur.prev), channel_id=1, source_target_pairs={{0,4},{1,3},{2,6},{3,1},{4,0},{5,9},{6,2},{7,11},{8,12},{9,5},{10,... | collective-permute-start | bytes 393224 | tf_op jit(solution)/shard_map/ppermute | solution.py:551
  10.8 3.0 %collective-permute-start.3 = (f32[4,64,128]{2,1,0:T(8,128)S(1)}, f32[4,64,128]{2,1,0:T(8,128)S(1)}, u32[]{:S(2)}, u32[]{:S(2)}) collective-permute-start(f32[4,64,128]{2,1,0:T(8,128)S(1)} %wave_halo.16.cur.prev), channel_id=1, source_target_pairs={{0,1},{1,0},{2,3},{3,2},{4,5},{5,4},{6,7},{7,6},{8,9},{9,8},{10,11... | collective-permute-start | bytes 393224 | tf_op jit(solution)/shard_map/ppermute | solution.py:555
  11.2 5.1 %collective-permute-start.4 = (f32[2,64,128]{2,1,0:T(8,128)S(1)}, f32[2,64,128]{2,1,0:T(8,128)S(1)}, u32[]{:S(2)}, u32[]{:S(2)}) collective-permute-start(f32[2,64,128]{2,1,0:T(8,128)S(1)} %get-tuple-element.125), channel_id=1, source_target_pairs={{0,4},{1,3},{2,6},{3,1},{4,0},{5,9},{6,2},{7,11},{8,12},{9,5},{10,... | collective-permute-start | bytes 196616 | tf_op jit(solution)/shard_map/ppermute | solution.py:551
  11.4 5.0 %collective-permute-start.5 = (f32[2,1,128]{2,1,0:T(1,128)S(1)}, f32[2,1,128]{2,1,0:T(1,128)S(1)}, u32[]{:S(2)}, u32[]{:S(2)}) collective-permute-start(f32[2,1,128]{2,1,0:T(1,128)S(1)} %get-tuple-element.127), channel_id=1, source_target_pairs={{0,1},{1,0},{2,3},{3,2},{4,5},{5,4},{6,7},{7,6},{8,9},{9,8},{10,11... | collective-permute-start | bytes 3080 | tf_op jit(solution)/shard_map/ppermute | solution.py:555
  13.8 5.0 %collective-permute-start.6 = (f32[4,64,128]{2,1,0:T(8,128)S(1)}, f32[4,64,128]{2,1,0:T(8,128)S(1)}, u32[]{:S(2)}, u32[]{:S(2)}) collective-permute-start(f32[4,64,128]{2,1,0:T(8,128)S(1)} %wave_halo.17.cur.prev), channel_id=1, source_target_pairs={{0,4},{1,3},{2,6},{3,1},{4,0},{5,9},{6,2},{7,11},{8,12},{9,5},{10,... | collective-permute-start | bytes 393224 | tf_op jit(solution)/shard_map/ppermute | solution.py:551
  16.4 5.2 %collective-permute-start.8 = (f32[2,2,128]{2,1,0:T(2,128)S(1)}, f32[2,2,128]{2,1,0:T(2,128)S(1)}, u32[]{:S(2)}, u32[]{:S(2)}) collective-permute-start(f32[2,2,128]{2,1,0:T(2,128)S(1)} %pad_maximum_fusion.1), channel_id=1, source_target_pairs={{0,2},{1,3},{2,0},{3,1},{4,6},{5,7},{6,4},{7,5},{8,10},{9,11},{10,... | collective-permute-start | bytes 6152 | tf_op jit(solution)/shard_map/ppermute | solution.py:555
  18.9 4.6 %collective-permute-start.10 = (f32[4,64,128]{2,1,0:T(8,128)S(1)}, f32[4,64,128]{2,1,0:T(8,128)S(1)}, u32[]{:S(2)}, u32[]{:S(2)}) collective-permute-start(f32[4,64,128]{2,1,0:T(8,128)S(1)} %wave_halo.18.cur.prev), channel_id=1, source_target_pairs={{0,1},{1,0},{2,3},{3,2},{4,5},{5,4},{6,7},{7,6},{8,9},{9,8},{10,11... | collective-permute-start | bytes 393224 | tf_op jit(solution)/shard_map/ppermute | solution.py:555
  19.0 6.1 %collective-permute-start.9 = (f32[4,64,128]{2,1,0:T(8,128)S(1)}, f32[4,64,128]{2,1,0:T(8,128)S(1)}, u32[]{:S(2)}, u32[]{:S(2)}) collective-permute-start(f32[4,64,128]{2,1,0:T(8,128)S(1)} %wave_halo.18.cur.prev), channel_id=1, source_target_pairs={{0,4},{1,3},{2,6},{3,1},{4,0},{5,9},{6,2},{7,11},{8,12},{9,5},{10,... | collective-permute-start | bytes 393224 | tf_op jit(solution)/shard_map/ppermute | solution.py:551
  25.2 5.5 %collective-permute-start.11 = (f32[4,64,128]{2,1,0:T(8,128)S(1)}, f32[4,64,128]{2,1,0:T(8,128)S(1)}, u32[]{:S(2)}, u32[]{:S(2)}) collective-permute-start(f32[4,64,128]{2,1,0:T(8,128)S(1)} %wave_halo.19.cur.prev), channel_id=1, source_target_pairs={{0,4},{1,3},{2,6},{3,1},{4,0},{5,9},{6,2},{7,11},{8,12},{9,5},{10,... | collective-permute-start | bytes 393224 | tf_op jit(solution)/shard_map/ppermute | solution.py:551
  30.7 5.2 %collective-permute-start.13 = (f32[4,64,128]{2,1,0:T(8,128)S(1)}, f32[4,64,128]{2,1,0:T(8,128)S(1)}, u32[]{:S(2)}, u32[]{:S(2)}) collective-permute-start(f32[4,64,128]{2,1,0:T(8,128)S(1)} %wave_halo.20.cur.prev), channel_id=1, source_target_pairs={{0,4},{1,3},{2,6},{3,1},{4,0},{5,9},{6,2},{7,11},{8,12},{9,5},{10,... | collective-permute-start | bytes 393224 | tf_op jit(solution)/shard_map/ppermute | solution.py:551
  36.0 5.0 %collective-permute-start.15 = (f32[4,64,128]{2,1,0:T(8,128)S(1)}, f32[4,64,128]{2,1,0:T(8,128)S(1)}, u32[]{:S(2)}, u32[]{:S(2)}) collective-permute-start(f32[4,64,128]{2,1,0:T(8,128)S(1)} %wave_halo.21.cur.prev), channel_id=1, source_target_pairs={{0,4},{1,3},{2,6},{3,1},{4,0},{5,9},{6,2},{7,11},{8,12},{9,5},{10,... | collective-permute-start | bytes 393224 | tf_op jit(solution)/shard_map/ppermute | solution.py:551
  41.1 5.0 %collective-permute-start.17 = (f32[4,64,128]{2,1,0:T(8,128)S(1)}, f32[4,64,128]{2,1,0:T(8,128)S(1)}, u32[]{:S(2)}, u32[]{:S(2)}) collective-permute-start(f32[4,64,128]{2,1,0:T(8,128)S(1)} %wave_halo.22.cur.prev), channel_id=1, source_target_pairs={{0,4},{1,3},{2,6},{3,1},{4,0},{5,9},{6,2},{7,11},{8,12},{9,5},{10,... | collective-permute-start | bytes 393224 | tf_op jit(solution)/shard_map/ppermute | solution.py:551
  46.2 5.0 %collective-permute-start.19 = (f32[4,64,128]{2,1,0:T(8,128)S(1)}, f32[4,64,128]{2,1,0:T(8,128)S(1)}, u32[]{:S(2)}, u32[]{:S(2)}) collective-permute-start(f32[4,64,128]{2,1,0:T(8,128)S(1)} %wave_halo.23.cur.prev), channel_id=1, source_target_pairs={{0,4},{1,3},{2,6},{3,1},{4,0},{5,9},{6,2},{7,11},{8,12},{9,5},{10,... | collective-permute-start | bytes 393224 | tf_op jit(solution)/shard_map/ppermute | solution.py:551
  51.3 5.0 %collective-permute-start.22 = (f32[4,64,128]{2,1,0:T(8,128)S(1)}, f32[4,64,128]{2,1,0:T(8,128)S(1)}, u32[]{:S(2)}, u32[]{:S(2)}) collective-permute-start(f32[4,64,128]{2,1,0:T(8,128)S(1)} %wave_halo.24.cur.prev), channel_id=1, source_target_pairs={{0,4},{1,3},{2,6},{3,1},{4,0},{5,9},{6,2},{7,11},{8,12},{9,5},{10,... | collective-permute-start | bytes 393224 | tf_op jit(solution)/shard_map/ppermute | solution.py:551
  56.4 5.0 %collective-permute-start.24 = (f32[4,64,128]{2,1,0:T(8,128)S(1)}, f32[4,64,128]{2,1,0:T(8,128)S(1)}, u32[]{:S(2)}, u32[]{:S(2)}) collective-permute-start(f32[4,64,128]{2,1,0:T(8,128)S(1)} %wave_halo.25.cur.prev), channel_id=1, source_target_pairs={{0,4},{1,3},{2,6},{3,1},{4,0},{5,9},{6,2},{7,11},{8,12},{9,5},{10,... | collective-permute-start | bytes 393224 | tf_op jit(solution)/shard_map/ppermute | solution.py:551
  61.5 5.3 %collective-permute-start.27 = (f32[4,64,128]{2,1,0:T(8,128)S(1)}, f32[4,64,128]{2,1,0:T(8,128)S(1)}, u32[]{:S(2)}, u32[]{:S(2)}) collective-permute-start(f32[4,64,128]{2,1,0:T(8,128)S(1)} %wave_halo.26.cur.prev), channel_id=1, source_target_pairs={{0,4},{1,3},{2,6},{3,1},{4,0},{5,9},{6,2},{7,11},{8,12},{9,5},{10,... | collective-permute-start | bytes 393224 | tf_op jit(solution)/shard_map/ppermute | solution.py:551
  66.9 5.5 %collective-permute-start.30 = (f32[4,64,128]{2,1,0:T(8,128)S(1)}, f32[4,64,128]{2,1,0:T(8,128)S(1)}, u32[]{:S(2)}, u32[]{:S(2)}) collective-permute-start(f32[4,64,128]{2,1,0:T(8,128)S(1)} %wave_halo.27.cur.prev), channel_id=1, source_target_pairs={{0,4},{1,3},{2,6},{3,1},{4,0},{5,9},{6,2},{7,11},{8,12},{9,5},{10,... | collective-permute-start | bytes 393224 | tf_op jit(solution)/shard_map/ppermute | solution.py:551
  69.0 3.4 %collective-permute-start.31 = (f32[4,64,128]{2,1,0:T(8,128)S(1)}, f32[4,64,128]{2,1,0:T(8,128)S(1)}, u32[]{:S(2)}, u32[]{:S(2)}) collective-permute-start(f32[4,64,128]{2,1,0:T(8,128)S(1)} %wave_halo.27.cur.prev), channel_id=1, source_target_pairs={{0,1},{1,0},{2,3},{3,2},{4,5},{5,4},{6,7},{7,6},{8,9},{9,8},{10,11... | collective-permute-start | bytes 393224 | tf_op jit(solution)/shard_map/ppermute | solution.py:555
  69.0 3.0 %collective-permute-start.29 = (f32[4,128]{1,0:T(4,128)S(1)}, f32[4,128]{1,0:T(4,128)S(1)}, u32[]{:S(2)}, u32[]{:S(2)}) collective-permute-start(f32[4,128]{1,0:T(4,128)S(1)} %shard_map.129.first), channel_id=1, source_target_pairs={{0,5},{1,4},{2,7},{3,6},{4,1},{5,0},{6,3},{7,2},{8,13},{9,12},{10,... | collective-permute-start | bytes 6152 | tf_op jit(solution)/shard_map/ppermute | solution.py:555
  72.5 11.4 %collective-permute-start.34 = (f32[4,64,128]{2,1,0:T(8,128)S(1)}, f32[4,64,128]{2,1,0:T(8,128)S(1)}, u32[]{:S(2)}, u32[]{:S(2)}) collective-permute-start(f32[4,64,128]{2,1,0:T(8,128)S(1)} %wave_halo.28.cur.prev), channel_id=1, source_target_pairs={{0,4},{1,3},{2,6},{3,1},{4,0},{5,9},{6,2},{7,11},{8,12},{9,5},{10,... | collective-permute-start | bytes 393224 | tf_op jit(solution)/shard_map/ppermute | solution.py:551
  74.1 9.8 %collective-permute-start.35 = (f32[4,64,128]{2,1,0:T(8,128)S(1)}, f32[4,64,128]{2,1,0:T(8,128)S(1)}, u32[]{:S(2)}, u32[]{:S(2)}) collective-permute-start(f32[4,64,128]{2,1,0:T(8,128)S(1)} %wave_halo.28.cur.prev), channel_id=1, source_target_pairs={{0,1},{1,0},{2,3},{3,2},{4,5},{5,4},{6,7},{7,6},{8,9},{9,8},{10,11... | collective-permute-start | bytes 393224 | tf_op jit(solution)/shard_map/ppermute | solution.py:555
  74.3 3.9 %collective-permute-start.32 = (f32[4,128]{1,0:T(4,128)S(1)}, f32[4,128]{1,0:T(4,128)S(1)}, u32[]{:S(2)}, u32[]{:S(2)}) collective-permute-start(f32[4,128]{1,0:T(4,128)S(1)} %shard_map.130.first), channel_id=1, source_target_pairs={{0,9},{1,8},{2,11},{3,10},{4,13},{5,12},{6,15},{7,14},{8,1},{9,0},... | collective-permute-start | bytes 6152 | tf_op jit(solution)/shard_map/ppermute | solution.py:555
  78.2 3.9 %collective-permute-start.33 = (f32[4,128]{1,0:T(4,128)S(1)}, f32[4,128]{1,0:T(4,128)S(1)}, u32[]{:S(2)}, u32[]{:S(2)}) collective-permute-start(f32[4,128]{1,0:T(4,128)S(1)} %shard_map.131.packed), channel_id=1, source_target_pairs={{0,17},{1,16},{2,19},{3,18},{4,21},{5,20},{6,23},{7,22},{8,25},{9,... | collective-permute-start | bytes 6152 | tf_op jit(solution)/shard_map/ppermute | solution.py:555
  84.0 5.8 %collective-permute-start.36 = (f32[4,64,128]{2,1,0:T(8,128)S(1)}, f32[4,64,128]{2,1,0:T(8,128)S(1)}, u32[]{:S(2)}, u32[]{:S(2)}) collective-permute-start(f32[4,64,128]{2,1,0:T(8,128)S(1)} %wave_halo.29.cur.prev), channel_id=1, source_target_pairs={{0,4},{1,3},{2,6},{3,1},{4,0},{5,9},{6,2},{7,11},{8,12},{9,5},{10,... | collective-permute-start | bytes 393224 | tf_op jit(solution)/shard_map/ppermute | solution.py:551
  85.9 3.9 %collective-permute-start.37 = (f32[4,64,128]{2,1,0:T(8,128)S(1)}, f32[4,64,128]{2,1,0:T(8,128)S(1)}, u32[]{:S(2)}, u32[]{:S(2)}) collective-permute-start(f32[4,64,128]{2,1,0:T(8,128)S(1)} %wave_halo.29.cur.prev), channel_id=1, source_target_pairs={{0,1},{1,0},{2,3},{3,2},{4,5},{5,4},{6,7},{7,6},{8,9},{9,8},{10,11... | collective-permute-start | bytes 393224 | tf_op jit(solution)/shard_map/ppermute | solution.py:555
  89.8 5.5 %collective-permute-start.38 = (f32[4,64,128]{2,1,0:T(8,128)S(1)}, f32[4,64,128]{2,1,0:T(8,128)S(1)}, u32[]{:S(2)}, u32[]{:S(2)}) collective-permute-start(f32[4,64,128]{2,1,0:T(8,128)S(1)} %wave_halo.30.cur), channel_id=1, source_target_pairs={{0,4},{1,3},{2,6},{3,1},{4,0},{5,9},{6,2},{7,11},{8,12},{9,5},{10,... | collective-permute-start | bytes 393224 | tf_op jit(solution)/shard_map/ppermute | solution.py:551
  95.4 6.6 %collective-permute-start.43 = (f32[4,64,128]{2,1,0:T(8,128)S(1)}, f32[4,64,128]{2,1,0:T(8,128)S(1)}, u32[]{:S(2)}, u32[]{:S(2)}) collective-permute-start(f32[4,64,128]{2,1,0:T(8,128)S(1)} %wave_halo.31.cur.own), channel_id=1, source_target_pairs={{0,1},{1,0},{2,3},{3,2},{4,5},{5,4},{6,7},{7,6},{8,9},{9,8},{10,11... | collective-permute-start | bytes 393224 | tf_op jit(solution)/shard_map/ppermute | solution.py:555
  97.2 3.5 %collective-permute-start.41 = (f32[32,128]{1,0:T(8,128)S(1)}, f32[32,128]{1,0:T(8,128)S(1)}, u32[]{:S(2)}, u32[]{:S(2)}) collective-permute-start(f32[32,128]{1,0:T(8,128)S(1)} %shard_map.133.first), channel_id=1, source_target_pairs={{0,5},{1,4},{2,7},{3,6},{4,1},{5,0},{6,3},{7,2},{8,13},{9,12},{10,... | collective-permute-start | bytes 49160 | tf_op jit(solution)/shard_map/ppermute | solution.py:555
  100.7 3.2 %collective-permute-start.42 = (f32[32,128]{1,0:T(8,128)S(1)}, f32[32,128]{1,0:T(8,128)S(1)}, u32[]{:S(2)}, u32[]{:S(2)}) collective-permute-start(f32[32,128]{1,0:T(8,128)S(1)} %shard_map.134.first), channel_id=1, source_target_pairs={{0,9},{1,8},{2,11},{3,10},{4,13},{5,12},{6,15},{7,14},{8,1},{9,0},... | collective-permute-start | bytes 49160 | tf_op jit(solution)/shard_map/ppermute | solution.py:555
  103.9 4.1 %collective-permute-start.44 = (f32[32,128]{1,0:T(8,128)S(1)}, f32[32,128]{1,0:T(8,128)S(1)}, u32[]{:S(2)}, u32[]{:S(2)}) collective-permute-start(f32[32,128]{1,0:T(8,128)S(1)} %shard_map.135.packed), channel_id=1, source_target_pairs={{0,17},{1,16},{2,19},{3,18},{4,21},{5,20},{6,23},{7,22},{8,25},{9,... | collective-permute-start | bytes 49160 | tf_op jit(solution)/shard_map/ppermute | solution.py:555
  (16 other events, 69.7 us)

commit v2 on v1

--- a/solution.py
+++ b/solution.py
@@ -631,11 +631,11 @@
         return "table"
 
     pieces = 5
-    part = -(-n_stations // (8 * pieces)) * 8
+    part = n_stations * 7 // 256 * 8
 
     def forward(i):
         def work(gate):
-            size = min(part, n_stations - i * part)
+            size = part if i < pieces - 1 else n_stations - i * part
             state[i] = gravity_forward(
                 i * part, size, 0, total_x, lateral, gate(state["head"]), state["table"], dens
             )
@@ -693,15 +693,15 @@
     hidden = chunks == 1 and count & (count - 1) == 0
     jobs = [exchange(1 << b) for b in range(stations.bit_length() - 1)]
     if hidden:
-        jobs += [build_table] + [forward(i) for i in range(pieces)] + [both(predict, cross)]
+        jobs += [build_table] + [forward(i) for i in range(pieces - 1)]
+        jobs += [both(share_edges, forward(pieces - 1)), both(predict, cross)]
         jobs += [add_up(1 << b) for b in range(count.bit_length() - 1)]
         quarter = lines // 4
         jobs += [both(residual, adjoint(range(quarter)))]
         jobs += [adjoint(range(quarter, 3 * quarter)), adjoint(range(3 * quarter, lines))]
     jobs[0] = both(send_edges, jobs[0])
-    jobs[1] = both(share_edges, jobs[1])
     if not hidden:
-        jobs.append(cross)
+        jobs += [share_edges, cross]
     assert len(jobs) < steps
 
     surf = cour

time: 109 us -> 110 us (level)
    ppermute x17, waiting for transfers between devices: 13.9 us -> 15.5 us  [across(): return lax.ppermute(value, AXES, chain)]
  transfers between devices with their start and end apart: 45 -> 45, of which waited for: 23 -> 23; matrix products, arithmetic and copies ran while one was open for 0% -> 0% of each run, Pallas kernels for 25% -> 24%
where the time goes in v2:
time: 110 us
  starting transfers between devices  51.8 us (47%)
  Pallas kernels  29.3 us (27%)
  waiting for transfers between devices  27.1 us (25%)
  between operations  1.74 us (2%)
    ppermute x17, starting transfers between devices, across(): return lax.ppermute(value, AXES, chain)  36.6 us
    ppermute x17, waiting for transfers between devices, across(): return lax.ppermute(value, AXES, chain)  15.5 us
    ppermute x28, starting transfers between devices, swap(): return lax.ppermute(value, AXES, pairs)  15.2 us
    ppermute x28, waiting for transfers between devices, swap(): return lax.ppermute(value, AXES, pairs)  11.6 us
    pallas_call x5, Pallas kernels, gravity_forward(): pl.pallas_call(functools.partial(forward_kernel, first, guard, total_x, l...  9.51 us
    pallas_call x16, Pallas kernels, local_step(): pl.pallas_call(functools.partial(local_kernel, step), out_shape=(shape(cu...  6.17 us
    pallas_call x3, Pallas kernels, gravity_adjoint(): pl.pallas_call(functools.partial(adjoint_kernel, lines, guard, total_x, l...  5.05 us
  transfers between devices with their start and end apart: 45, of which 23 were waited for; matrix products, arithmetic and copies ran while one was open for 0% of the time, Pallas kernels for 24%

profile of v2, /device:TPU:0, one launch (start us, length us, event | category | flops | bytes accessed | tf_op | source)
XLA Modules:
  0.0 110.1 jit_solution(7186042091572916937)
XLA Ops:
  1.5 3.0 %collective-permute-start = (f32[4,64,128]{2,1,0:T(8,128)S(1)}, f32[4,64,128]{2,1,0:T(8,128)S(1)}, u32[]{:S(2)}, u32[]{:S(2)}) collective-permute-start(f32[4,64,128]{2,1,0:T(8,128)S(1)} %first_planes.1.cur.prev), channel_id=1, source_target_pairs={{0,4},{1,3},{2,6},{3,1},{4,0},{5,9},{6,2},{7,11},{8,12},{9,5},{10,... | collective-permute-start | bytes 393224 | tf_op jit(solution)/shard_map/ppermute | solution.py:551
  8.3 2.5 %collective-permute-start.2 = (f32[4,64,128]{2,1,0:T(8,128)S(1)}, f32[4,64,128]{2,1,0:T(8,128)S(1)}, u32[]{:S(2)}, u32[]{:S(2)}) collective-permute-start(f32[4,64,128]{2,1,0:T(8,128)S(1)} %wave_halo.16.cur.prev), channel_id=1, source_target_pairs={{0,4},{1,3},{2,6},{3,1},{4,0},{5,9},{6,2},{7,11},{8,12},{9,5},{10,... | collective-permute-start | bytes 393224 | tf_op jit(solution)/shard_map/ppermute | solution.py:551
  11.8 2.0 %collective-permute-done.2.outer = f32[4,64,128]{2,1,0:T(8,128)S(1)} collective-permute-done((f32[4,64,128]{2,1,0:T(8,128)S(1)}, f32[4,64,128]{2,1,0:T(8,128)S(1)}, u32[]{:S(2)}, u32[]{:S(2)}) %collective-permute-start.2) | collective-permute-done | bytes 131104 | tf_op jit(solution)/shard_map/ppermute | solution.py:551
  13.8 2.1 %collective-permute-start.5 = (f32[4,64,128]{2,1,0:T(8,128)S(1)}, f32[4,64,128]{2,1,0:T(8,128)S(1)}, u32[]{:S(2)}, u32[]{:S(2)}) collective-permute-start(f32[4,64,128]{2,1,0:T(8,128)S(1)} %wave_halo.17.cur.prev), channel_id=1, source_target_pairs={{0,4},{1,3},{2,6},{3,1},{4,0},{5,9},{6,2},{7,11},{8,12},{9,5},{10,... | collective-permute-start | bytes 393224 | tf_op jit(solution)/shard_map/ppermute | solution.py:551
  18.9 2.1 %collective-permute-start.8 = (f32[4,64,128]{2,1,0:T(8,128)S(1)}, f32[4,64,128]{2,1,0:T(8,128)S(1)}, u32[]{:S(2)}, u32[]{:S(2)}) collective-permute-start(f32[4,64,128]{2,1,0:T(8,128)S(1)} %wave_halo.18.cur.prev), channel_id=1, source_target_pairs={{0,4},{1,3},{2,6},{3,1},{4,0},{5,9},{6,2},{7,11},{8,12},{9,5},{10,... | collective-permute-start | bytes 393224 | tf_op jit(solution)/shard_map/ppermute | solution.py:551
  21.5 1.8 %gravity_table.1.table = f32[9088,128]{1,0:T(8,128)S(1)} custom-call(s32[1]{0:T(128)} %constant.54.clone.1.head), custom_call_target="tpu_custom_call" | custom-call | flops 23265280 | bytes 4653056 | tf_op jit(solution)/shard_map/gravity_table/pallas_call | solution.py:346
  24.0 2.1 %collective-permute-start.10 = (f32[4,64,128]{2,1,0:T(8,128)S(1)}, f32[4,64,128]{2,1,0:T(8,128)S(1)}, u32[]{:S(2)}, u32[]{:S(2)}) collective-permute-start(f32[4,64,128]{2,1,0:T(8,128)S(1)} %wave_halo.19.cur.prev), channel_id=1, source_target_pairs={{0,4},{1,3},{2,6},{3,1},{4,0},{5,9},{6,2},{7,11},{8,12},{9,5},{10,... | collective-permute-start | bytes 393224 | tf_op jit(solution)/shard_map/ppermute | solution.py:551
  26.5 2.0 %gravity_forward.5.refs_0_ = f32[112,128]{1,0:T(8,128)S(1)} custom-call(s32[513]{0:T(1024)S(1)} %pad_add_fusion.head, f32[9088,128]{1,0:T(8,128)S(1)} %gravity_table.1.table, f32[4,64,128]{2,1,0:T(8,128)S(1)} %get-tuple-element.141.dens), custom_call_target="tpu_custom_call" | custom-call | flops 14680064 | bytes 131072 | tf_op jit(solution)/shard_map/gravity_forward/pallas_call | solution.py:391
  29.1 2.1 %collective-permute-start.12 = (f32[4,64,128]{2,1,0:T(8,128)S(1)}, f32[4,64,128]{2,1,0:T(8,128)S(1)}, u32[]{:S(2)}, u32[]{:S(2)}) collective-permute-start(f32[4,64,128]{2,1,0:T(8,128)S(1)} %wave_halo.20.cur.prev), channel_id=1, source_target_pairs={{0,4},{1,3},{2,6},{3,1},{4,0},{5,9},{6,2},{7,11},{8,12},{9,5},{10,... | collective-permute-start | bytes 393224 | tf_op jit(solution)/shard_map/ppermute | solution.py:551
  31.6 2.0 %gravity_forward.6.refs_1_ = f32[112,128]{1,0:T(8,128)S(1)} custom-call(s32[513]{0:T(1024)S(1)} %pad_add_fusion.head, f32[9088,128]{1,0:T(8,128)S(1)} %gravity_table.1.table, f32[4,64,128]{2,1,0:T(8,128)S(1)} %get-tuple-element.141.dens), custom_call_target="tpu_custom_call" | custom-call | flops 14680064 | bytes 131072 | tf_op jit(solution)/shard_map/gravity_forward/pallas_call | solution.py:391
  34.2 2.1 %collective-permute-start.14 = (f32[4,64,128]{2,1,0:T(8,128)S(1)}, f32[4,64,128]{2,1,0:T(8,128)S(1)}, u32[]{:S(2)}, u32[]{:S(2)}) collective-permute-start(f32[4,64,128]{2,1,0:T(8,128)S(1)} %wave_halo.21.cur.prev), channel_id=1, source_target_pairs={{0,4},{1,3},{2,6},{3,1},{4,0},{5,9},{6,2},{7,11},{8,12},{9,5},{10,... | collective-permute-start | bytes 393224 | tf_op jit(solution)/shard_map/ppermute | solution.py:551
  36.7 2.0 %gravity_forward.7.refs_2_ = f32[112,128]{1,0:T(8,128)S(1)} custom-call(s32[513]{0:T(1024)S(1)} %pad_add_fusion.head, f32[9088,128]{1,0:T(8,128)S(1)} %gravity_table.1.table, f32[4,64,128]{2,1,0:T(8,128)S(1)} %get-tuple-element.141.dens), custom_call_target="tpu_custom_call" | custom-call | flops 14680064 | bytes 131072 | tf_op jit(solution)/shard_map/gravity_forward/pallas_call | solution.py:391
  39.3 2.1 %collective-permute-start.16 = (f32[4,64,128]{2,1,0:T(8,128)S(1)}, f32[4,64,128]{2,1,0:T(8,128)S(1)}, u32[]{:S(2)}, u32[]{:S(2)}) collective-permute-start(f32[4,64,128]{2,1,0:T(8,128)S(1)} %wave_halo.22.cur.prev), channel_id=1, source_target_pairs={{0,4},{1,3},{2,6},{3,1},{4,0},{5,9},{6,2},{7,11},{8,12},{9,5},{10,... | collective-permute-start | bytes 393224 | tf_op jit(solution)/shard_map/ppermute | solution.py:551
  41.8 2.0 %gravity_forward.8.refs_3_ = f32[112,128]{1,0:T(8,128)S(1)} custom-call(s32[513]{0:T(1024)S(1)} %pad_add_fusion.head, f32[9088,128]{1,0:T(8,128)S(1)} %gravity_table.1.table, f32[4,64,128]{2,1,0:T(8,128)S(1)} %get-tuple-element.141.dens), custom_call_target="tpu_custom_call" | custom-call | flops 14680064 | bytes 131072 | tf_op jit(solution)/shard_map/gravity_forward/pallas_call | solution.py:391
  44.5 2.1 %collective-permute-start.19 = (f32[4,64,128]{2,1,0:T(8,128)S(1)}, f32[4,64,128]{2,1,0:T(8,128)S(1)}, u32[]{:S(2)}, u32[]{:S(2)}) collective-permute-start(f32[4,64,128]{2,1,0:T(8,128)S(1)} %wave_halo.23.cur.prev), channel_id=1, source_target_pairs={{0,4},{1,3},{2,6},{3,1},{4,0},{5,9},{6,2},{7,11},{8,12},{9,5},{10,... | collective-permute-start | bytes 393224 | tf_op jit(solution)/shard_map/ppermute | solution.py:551
  48.2 2.6 %collective-permute-done.18.outer = f32[2,64,128]{2,1,0:T(8,128)S(1)} collective-permute-done((f32[2,64,128]{2,1,0:T(8,128)S(1)}, f32[2,64,128]{2,1,0:T(8,128)S(1)}, u32[]{:S(2)}, u32[]{:S(2)}) %collective-permute-start.18) | collective-permute-done | bytes 65568 | tf_op jit(solution)/shard_map/ppermute | solution.py:551
  52.3 2.4 %collective-permute-start.22 = (f32[4,64,128]{2,1,0:T(8,128)S(1)}, f32[4,64,128]{2,1,0:T(8,128)S(1)}, u32[]{:S(2)}, u32[]{:S(2)}) collective-permute-start(f32[4,64,128]{2,1,0:T(8,128)S(1)} %wave_halo.24.cur.prev), channel_id=1, source_target_pairs={{0,4},{1,3},{2,6},{3,1},{4,0},{5,9},{6,2},{7,11},{8,12},{9,5},{10,... | collective-permute-start | bytes 393224 | tf_op jit(solution)/shard_map/ppermute | solution.py:551
  57.8 2.5 %collective-permute-start.24 = (f32[4,64,128]{2,1,0:T(8,128)S(1)}, f32[4,64,128]{2,1,0:T(8,128)S(1)}, u32[]{:S(2)}, u32[]{:S(2)}) collective-permute-start(f32[4,64,128]{2,1,0:T(8,128)S(1)} %wave_halo.25.cur.prev), channel_id=1, source_target_pairs={{0,4},{1,3},{2,6},{3,1},{4,0},{5,9},{6,2},{7,11},{8,12},{9,5},{10,... | collective-permute-start | bytes 393224 | tf_op jit(solution)/shard_map/ppermute | solution.py:551
  60.8 2.4 %collective-permute-done.24.outer = f32[4,64,128]{2,1,0:T(8,128)S(1)} collective-permute-done((f32[4,64,128]{2,1,0:T(8,128)S(1)}, f32[4,64,128]{2,1,0:T(8,128)S(1)}, u32[]{:S(2)}, u32[]{:S(2)}) %collective-permute-start.24) | collective-permute-done | bytes 131104 | tf_op jit(solution)/shard_map/ppermute | solution.py:551
  63.2 2.2 %collective-permute-start.27 = (f32[4,64,128]{2,1,0:T(8,128)S(1)}, f32[4,64,128]{2,1,0:T(8,128)S(1)}, u32[]{:S(2)}, u32[]{:S(2)}) collective-permute-start(f32[4,64,128]{2,1,0:T(8,128)S(1)} %wave_halo.26.cur.prev), channel_id=1, source_target_pairs={{0,4},{1,3},{2,6},{3,1},{4,0},{5,9},{6,2},{7,11},{8,12},{9,5},{10,... | collective-permute-start | bytes 393224 | tf_op jit(solution)/shard_map/ppermute | solution.py:551
  68.5 2.1 %collective-permute-start.30 = (f32[4,64,128]{2,1,0:T(8,128)S(1)}, f32[4,64,128]{2,1,0:T(8,128)S(1)}, u32[]{:S(2)}, u32[]{:S(2)}) collective-permute-start(f32[4,64,128]{2,1,0:T(8,128)S(1)} %wave_halo.27.cur.prev), channel_id=1, source_target_pairs={{0,4},{1,3},{2,6},{3,1},{4,0},{5,9},{6,2},{7,11},{8,12},{9,5},{10,... | collective-permute-start | bytes 393224 | tf_op jit(solution)/shard_map/ppermute | solution.py:551
  70.7 2.8 %collective-permute-done.29.second = f32[4,128]{1,0:T(4,128)S(1)} collective-permute-done((f32[4,128]{1,0:T(4,128)S(1)}, f32[4,128]{1,0:T(4,128)S(1)}, u32[]{:S(2)}, u32[]{:S(2)}) %collective-permute-start.29) | collective-permute-done | bytes 2080 | tf_op jit(solution)/shard_map/ppermute | solution.py:555
  74.1 1.6 %collective-permute-start.34 = (f32[4,64,128]{2,1,0:T(8,128)S(1)}, f32[4,64,128]{2,1,0:T(8,128)S(1)}, u32[]{:S(2)}, u32[]{:S(2)}) collective-permute-start(f32[4,64,128]{2,1,0:T(8,128)S(1)} %wave_halo.28.cur.prev), channel_id=1, source_target_pairs={{0,4},{1,3},{2,6},{3,1},{4,0},{5,9},{6,2},{7,11},{8,12},{9,5},{10,... | collective-permute-start | bytes 393224 | tf_op jit(solution)/shard_map/ppermute | solution.py:551
  75.9 2.0 %collective-permute-start.32 = (f32[4,128]{1,0:T(4,128)S(1)}, f32[4,128]{1,0:T(4,128)S(1)}, u32[]{:S(2)}, u32[]{:S(2)}) collective-permute-start(f32[4,128]{1,0:T(4,128)S(1)} %shard_map.130.first), channel_id=1, source_target_pairs={{0,9},{1,8},{2,11},{3,10},{4,13},{5,12},{6,15},{7,14},{8,1},{9,0},... | collective-permute-start | bytes 6152 | tf_op jit(solution)/shard_map/ppermute | solution.py:555
  77.9 1.8 %collective-permute-done.32.second = f32[4,128]{1,0:T(4,128)S(1)} collective-permute-done((f32[4,128]{1,0:T(4,128)S(1)}, f32[4,128]{1,0:T(4,128)S(1)}, u32[]{:S(2)}, u32[]{:S(2)}) %collective-permute-start.32) | collective-permute-done | bytes 2080 | tf_op jit(solution)/shard_map/ppermute | solution.py:555
  79.7 2.5 %collective-permute-start.33 = (f32[4,128]{1,0:T(4,128)S(1)}, f32[4,128]{1,0:T(4,128)S(1)}, u32[]{:S(2)}, u32[]{:S(2)}) collective-permute-start(f32[4,128]{1,0:T(4,128)S(1)} %shard_map.131.packed), channel_id=1, source_target_pairs={{0,17},{1,16},{2,19},{3,18},{4,21},{5,20},{6,23},{7,22},{8,25},{9,... | collective-permute-start | bytes 6152 | tf_op jit(solution)/shard_map/ppermute | solution.py:555
  85.5 1.8 %collective-permute-start.36 = (f32[4,64,128]{2,1,0:T(8,128)S(1)}, f32[4,64,128]{2,1,0:T(8,128)S(1)}, u32[]{:S(2)}, u32[]{:S(2)}) collective-permute-start(f32[4,64,128]{2,1,0:T(8,128)S(1)} %wave_halo.29.cur.prev), channel_id=1, source_target_pairs={{0,4},{1,3},{2,6},{3,1},{4,0},{5,9},{6,2},{7,11},{8,12},{9,5},{10,... | collective-permute-start | bytes 393224 | tf_op jit(solution)/shard_map/ppermute | solution.py:551
  87.8 1.9 %gravity_adjoint.4.start_at = f32[8,16,128]{2,1,0:T(8,128)S(1)} custom-call(s32[513]{0:T(1024)S(1)} %pad_add_fusion.head, f32[4,128]{1,0:T(4,128)S(1)} %get-tuple-element.208.weights, f32[9088,128]{1,0:T(8,128)S(1)} %gravity_table.1.table, f32[8,16,128]{2,1,0:T(8,128)S(1)} %gravity_adjoint.3.start_at), custom_call_target="tpu_custom_call" | custom-call | flops 8388608 | bytes 131072 | tf_op jit(solution)/shard_map/gravity_adjoint/pallas_call | solution.py:431
  91.3 2.5 %collective-permute-start.38 = (f32[4,64,128]{2,1,0:T(8,128)S(1)}, f32[4,64,128]{2,1,0:T(8,128)S(1)}, u32[]{:S(2)}, u32[]{:S(2)}) collective-permute-start(f32[4,64,128]{2,1,0:T(8,128)S(1)} %wave_halo.30.cur), channel_id=1, source_target_pairs={{0,4},{1,3},{2,6},{3,1},{4,0},{5,9},{6,2},{7,11},{8,12},{9,5},{10,... | collective-permute-start | bytes 393224 | tf_op jit(solution)/shard_map/ppermute | solution.py:551
  94.2 1.9 %gravity_adjoint.5 = f32[8,16,128]{2,1,0:T(8,128)} custom-call(s32[513]{0:T(1024)S(1)} %pad_add_fusion.head, f32[4,128]{1,0:T(4,128)S(1)} %get-tuple-element.208.weights, f32[9088,128]{1,0:T(8,128)S(1)} %gravity_table.1.table, f32[8,16,128]{2,1,0:T(8,128)S(1)} %gravity_adjoint.4.start_at), custom_call_target="tpu_custom_call" | custom-call | flops 4194304 | bytes 131072 | tf_op jit(solution)/shard_map/gravity_adjoint/pallas_call | solution.py:431
  98.7 2.0 %collective-permute-start.41 = (f32[32,128]{1,0:T(8,128)S(1)}, f32[32,128]{1,0:T(8,128)S(1)}, u32[]{:S(2)}, u32[]{:S(2)}) collective-permute-start(f32[32,128]{1,0:T(8,128)S(1)} %shard_map.133.first), channel_id=1, source_target_pairs={{0,5},{1,4},{2,7},{3,6},{4,1},{5,0},{6,3},{7,2},{8,13},{9,12},{10,... | collective-permute-start | bytes 49160 | tf_op jit(solution)/shard_map/ppermute | solution.py:555
  105.3 2.7 %collective-permute-start.44 = (f32[32,128]{1,0:T(8,128)S(1)}, f32[32,128]{1,0:T(8,128)S(1)}, u32[]{:S(2)}, u32[]{:S(2)}) collective-permute-start(f32[32,128]{1,0:T(8,128)S(1)} %shard_map.135.packed), channel_id=1, source_target_pairs={{0,17},{1,16},{2,19},{3,18},{4,21},{5,20},{6,23},{7,22},{8,25},{9,... | collective-permute-start | bytes 49160 | tf_op jit(solution)/shard_map/ppermute | solution.py:555
  (126 shorter events, 38.5 us)
Async XLA Ops:
  1.5 6.7 %collective-permute-start = (f32[4,64,128]{2,1,0:T(8,128)S(1)}, f32[4,64,128]{2,1,0:T(8,128)S(1)}, u32[]{:S(2)}, u32[]{:S(2)}) collective-permute-start(f32[4,64,128]{2,1,0:T(8,128)S(1)} %first_planes.1.cur.prev), channel_id=1, source_target_pairs={{0,4},{1,3},{2,6},{3,1},{4,0},{5,9},{6,2},{7,11},{8,12},{9,5},{10,... | collective-permute-start | bytes 393224 | tf_op jit(solution)/shard_map/ppermute | solution.py:551
  4.5 3.7 %collective-permute-start.1 = (f32[4,64,128]{2,1,0:T(8,128)S(1)}, f32[4,64,128]{2,1,0:T(8,128)S(1)}, u32[]{:S(2)}, u32[]{:S(2)}) collective-permute-start(f32[4,64,128]{2,1,0:T(8,128)S(1)} %first_planes.1.cur.prev), channel_id=1, source_target_pairs={{0,1},{1,0},{2,3},{3,2},{4,5},{5,4},{6,7},{7,6},{8,9},{9,8},{10,11... | collective-permute-start | bytes 393224 | tf_op jit(solution)/shard_map/ppermute | solution.py:555
  8.3 5.5 %collective-permute-start.2 = (f32[4,64,128]{2,1,0:T(8,128)S(1)}, f32[4,64,128]{2,1,0:T(8,128)S(1)}, u32[]{:S(2)}, u32[]{:S(2)}) collective-permute-start(f32[4,64,128]{2,1,0:T(8,128)S(1)} %wave_halo.16.cur.prev), channel_id=1, source_target_pairs={{0,4},{1,3},{2,6},{3,1},{4,0},{5,9},{6,2},{7,11},{8,12},{9,5},{10,... | collective-permute-start | bytes 393224 | tf_op jit(solution)/shard_map/ppermute | solution.py:551
  10.8 3.0 %collective-permute-start.3 = (f32[4,64,128]{2,1,0:T(8,128)S(1)}, f32[4,64,128]{2,1,0:T(8,128)S(1)}, u32[]{:S(2)}, u32[]{:S(2)}) collective-permute-start(f32[4,64,128]{2,1,0:T(8,128)S(1)} %wave_halo.16.cur.prev), channel_id=1, source_target_pairs={{0,1},{1,0},{2,3},{3,2},{4,5},{5,4},{6,7},{7,6},{8,9},{9,8},{10,11... | collective-permute-start | bytes 393224 | tf_op jit(solution)/shard_map/ppermute | solution.py:555
  11.2 5.1 %collective-permute-start.4 = (f32[2,1,128]{2,1,0:T(1,128)S(1)}, f32[2,1,128]{2,1,0:T(1,128)S(1)}, u32[]{:S(2)}, u32[]{:S(2)}) collective-permute-start(f32[2,1,128]{2,1,0:T(1,128)S(1)} %get-tuple-element.125), channel_id=1, source_target_pairs={{0,1},{1,0},{2,3},{3,2},{4,5},{5,4},{6,7},{7,6},{8,9},{9,8},{10,11... | collective-permute-start | bytes 3080 | tf_op jit(solution)/shard_map/ppermute | solution.py:555
  13.8 5.0 %collective-permute-start.5 = (f32[4,64,128]{2,1,0:T(8,128)S(1)}, f32[4,64,128]{2,1,0:T(8,128)S(1)}, u32[]{:S(2)}, u32[]{:S(2)}) collective-permute-start(f32[4,64,128]{2,1,0:T(8,128)S(1)} %wave_halo.17.cur.prev), channel_id=1, source_target_pairs={{0,4},{1,3},{2,6},{3,1},{4,0},{5,9},{6,2},{7,11},{8,12},{9,5},{10,... | collective-permute-start | bytes 393224 | tf_op jit(solution)/shard_map/ppermute | solution.py:551
  16.4 5.1 %collective-permute-start.7 = (f32[2,2,128]{2,1,0:T(2,128)S(1)}, f32[2,2,128]{2,1,0:T(2,128)S(1)}, u32[]{:S(2)}, u32[]{:S(2)}) collective-permute-start(f32[2,2,128]{2,1,0:T(2,128)S(1)} %pad_maximum_fusion.1), channel_id=1, source_target_pairs={{0,2},{1,3},{2,0},{3,1},{4,6},{5,7},{6,4},{7,5},{8,10},{9,11},{10,... | collective-permute-start | bytes 6152 | tf_op jit(solution)/shard_map/ppermute | solution.py:555
  18.9 5.0 %collective-permute-start.8 = (f32[4,64,128]{2,1,0:T(8,128)S(1)}, f32[4,64,128]{2,1,0:T(8,128)S(1)}, u32[]{:S(2)}, u32[]{:S(2)}) collective-permute-start(f32[4,64,128]{2,1,0:T(8,128)S(1)} %wave_halo.18.cur.prev), channel_id=1, source_target_pairs={{0,4},{1,3},{2,6},{3,1},{4,0},{5,9},{6,2},{7,11},{8,12},{9,5},{10,... | collective-permute-start | bytes 393224 | tf_op jit(solution)/shard_map/ppermute | solution.py:551
  24.0 5.0 %collective-permute-start.10 = (f32[4,64,128]{2,1,0:T(8,128)S(1)}, f32[4,64,128]{2,1,0:T(8,128)S(1)}, u32[]{:S(2)}, u32[]{:S(2)}) collective-permute-start(f32[4,64,128]{2,1,0:T(8,128)S(1)} %wave_halo.19.cur.prev), channel_id=1, source_target_pairs={{0,4},{1,3},{2,6},{3,1},{4,0},{5,9},{6,2},{7,11},{8,12},{9,5},{10,... | collective-permute-start | bytes 393224 | tf_op jit(solution)/shard_map/ppermute | solution.py:551
  29.1 5.0 %collective-permute-start.12 = (f32[4,64,128]{2,1,0:T(8,128)S(1)}, f32[4,64,128]{2,1,0:T(8,128)S(1)}, u32[]{:S(2)}, u32[]{:S(2)}) collective-permute-start(f32[4,64,128]{2,1,0:T(8,128)S(1)} %wave_halo.20.cur.prev), channel_id=1, source_target_pairs={{0,4},{1,3},{2,6},{3,1},{4,0},{5,9},{6,2},{7,11},{8,12},{9,5},{10,... | collective-permute-start | bytes 393224 | tf_op jit(solution)/shard_map/ppermute | solution.py:551
  34.2 5.0 %collective-permute-start.14 = (f32[4,64,128]{2,1,0:T(8,128)S(1)}, f32[4,64,128]{2,1,0:T(8,128)S(1)}, u32[]{:S(2)}, u32[]{:S(2)}) collective-permute-start(f32[4,64,128]{2,1,0:T(8,128)S(1)} %wave_halo.21.cur.prev), channel_id=1, source_target_pairs={{0,4},{1,3},{2,6},{3,1},{4,0},{5,9},{6,2},{7,11},{8,12},{9,5},{10,... | collective-permute-start | bytes 393224 | tf_op jit(solution)/shard_map/ppermute | solution.py:551
  39.3 5.0 %collective-permute-start.16 = (f32[4,64,128]{2,1,0:T(8,128)S(1)}, f32[4,64,128]{2,1,0:T(8,128)S(1)}, u32[]{:S(2)}, u32[]{:S(2)}) collective-permute-start(f32[4,64,128]{2,1,0:T(8,128)S(1)} %wave_halo.22.cur.prev), channel_id=1, source_target_pairs={{0,4},{1,3},{2,6},{3,1},{4,0},{5,9},{6,2},{7,11},{8,12},{9,5},{10,... | collective-permute-start | bytes 393224 | tf_op jit(solution)/shard_map/ppermute | solution.py:551
  44.5 7.8 %collective-permute-start.19 = (f32[4,64,128]{2,1,0:T(8,128)S(1)}, f32[4,64,128]{2,1,0:T(8,128)S(1)}, u32[]{:S(2)}, u32[]{:S(2)}) collective-permute-start(f32[4,64,128]{2,1,0:T(8,128)S(1)} %wave_halo.23.cur.prev), channel_id=1, source_target_pairs={{0,4},{1,3},{2,6},{3,1},{4,0},{5,9},{6,2},{7,11},{8,12},{9,5},{10,... | collective-permute-start | bytes 393224 | tf_op jit(solution)/shard_map/ppermute | solution.py:551
  46.5 5.7 %collective-permute-start.20 = (f32[4,64,128]{2,1,0:T(8,128)S(1)}, f32[4,64,128]{2,1,0:T(8,128)S(1)}, u32[]{:S(2)}, u32[]{:S(2)}) collective-permute-start(f32[4,64,128]{2,1,0:T(8,128)S(1)} %wave_halo.23.cur.prev), channel_id=1, source_target_pairs={{0,1},{1,0},{2,3},{3,2},{4,5},{5,4},{6,7},{7,6},{8,9},{9,8},{10,11... | collective-permute-start | bytes 393224 | tf_op jit(solution)/shard_map/ppermute | solution.py:555
  46.5 4.3 %collective-permute-start.18 = (f32[2,64,128]{2,1,0:T(8,128)S(1)}, f32[2,64,128]{2,1,0:T(8,128)S(1)}, u32[]{:S(2)}, u32[]{:S(2)}) collective-permute-start(f32[2,64,128]{2,1,0:T(8,128)S(1)} %get-tuple-element.160), channel_id=1, source_target_pairs={{0,4},{1,3},{2,6},{3,1},{4,0},{5,9},{6,2},{7,11},{8,12},{9,5},{10,... | collective-permute-start | bytes 196616 | tf_op jit(solution)/shard_map/ppermute | solution.py:551
  52.3 5.4 %collective-permute-start.22 = (f32[4,64,128]{2,1,0:T(8,128)S(1)}, f32[4,64,128]{2,1,0:T(8,128)S(1)}, u32[]{:S(2)}, u32[]{:S(2)}) collective-permute-start(f32[4,64,128]{2,1,0:T(8,128)S(1)} %wave_halo.24.cur.prev), channel_id=1, source_target_pairs={{0,4},{1,3},{2,6},{3,1},{4,0},{5,9},{6,2},{7,11},{8,12},{9,5},{10,... | collective-permute-start | bytes 393224 | tf_op jit(solution)/shard_map/ppermute | solution.py:551
  57.8 5.4 %collective-permute-start.24 = (f32[4,64,128]{2,1,0:T(8,128)S(1)}, f32[4,64,128]{2,1,0:T(8,128)S(1)}, u32[]{:S(2)}, u32[]{:S(2)}) collective-permute-start(f32[4,64,128]{2,1,0:T(8,128)S(1)} %wave_halo.25.cur.prev), channel_id=1, source_target_pairs={{0,4},{1,3},{2,6},{3,1},{4,0},{5,9},{6,2},{7,11},{8,12},{9,5},{10,... | collective-permute-start | bytes 393224 | tf_op jit(solution)/shard_map/ppermute | solution.py:551
  63.2 5.1 %collective-permute-start.27 = (f32[4,64,128]{2,1,0:T(8,128)S(1)}, f32[4,64,128]{2,1,0:T(8,128)S(1)}, u32[]{:S(2)}, u32[]{:S(2)}) collective-permute-start(f32[4,64,128]{2,1,0:T(8,128)S(1)} %wave_halo.26.cur.prev), channel_id=1, source_target_pairs={{0,4},{1,3},{2,6},{3,1},{4,0},{5,9},{6,2},{7,11},{8,12},{9,5},{10,... | collective-permute-start | bytes 393224 | tf_op jit(solution)/shard_map/ppermute | solution.py:551
  68.5 5.5 %collective-permute-start.30 = (f32[4,64,128]{2,1,0:T(8,128)S(1)}, f32[4,64,128]{2,1,0:T(8,128)S(1)}, u32[]{:S(2)}, u32[]{:S(2)}) collective-permute-start(f32[4,64,128]{2,1,0:T(8,128)S(1)} %wave_halo.27.cur.prev), channel_id=1, source_target_pairs={{0,4},{1,3},{2,6},{3,1},{4,0},{5,9},{6,2},{7,11},{8,12},{9,5},{10,... | collective-permute-start | bytes 393224 | tf_op jit(solution)/shard_map/ppermute | solution.py:551
  70.5 3.4 %collective-permute-start.31 = (f32[4,64,128]{2,1,0:T(8,128)S(1)}, f32[4,64,128]{2,1,0:T(8,128)S(1)}, u32[]{:S(2)}, u32[]{:S(2)}) collective-permute-start(f32[4,64,128]{2,1,0:T(8,128)S(1)} %wave_halo.27.cur.prev), channel_id=1, source_target_pairs={{0,1},{1,0},{2,3},{3,2},{4,5},{5,4},{6,7},{7,6},{8,9},{9,8},{10,11... | collective-permute-start | bytes 393224 | tf_op jit(solution)/shard_map/ppermute | solution.py:555
  70.6 3.0 %collective-permute-start.29 = (f32[4,128]{1,0:T(4,128)S(1)}, f32[4,128]{1,0:T(4,128)S(1)}, u32[]{:S(2)}, u32[]{:S(2)}) collective-permute-start(f32[4,128]{1,0:T(4,128)S(1)} %shard_map.129.first), channel_id=1, source_target_pairs={{0,5},{1,4},{2,7},{3,6},{4,1},{5,0},{6,3},{7,2},{8,13},{9,12},{10,... | collective-permute-start | bytes 6152 | tf_op jit(solution)/shard_map/ppermute | solution.py:555
  74.1 11.4 %collective-permute-start.34 = (f32[4,64,128]{2,1,0:T(8,128)S(1)}, f32[4,64,128]{2,1,0:T(8,128)S(1)}, u32[]{:S(2)}, u32[]{:S(2)}) collective-permute-start(f32[4,64,128]{2,1,0:T(8,128)S(1)} %wave_halo.28.cur.prev), channel_id=1, source_target_pairs={{0,4},{1,3},{2,6},{3,1},{4,0},{5,9},{6,2},{7,11},{8,12},{9,5},{10,... | collective-permute-start | bytes 393224 | tf_op jit(solution)/shard_map/ppermute | solution.py:551
  75.7 9.8 %collective-permute-start.35 = (f32[4,64,128]{2,1,0:T(8,128)S(1)}, f32[4,64,128]{2,1,0:T(8,128)S(1)}, u32[]{:S(2)}, u32[]{:S(2)}) collective-permute-start(f32[4,64,128]{2,1,0:T(8,128)S(1)} %wave_halo.28.cur.prev), channel_id=1, source_target_pairs={{0,1},{1,0},{2,3},{3,2},{4,5},{5,4},{6,7},{7,6},{8,9},{9,8},{10,11... | collective-permute-start | bytes 393224 | tf_op jit(solution)/shard_map/ppermute | solution.py:555
  75.9 3.8 %collective-permute-start.32 = (f32[4,128]{1,0:T(4,128)S(1)}, f32[4,128]{1,0:T(4,128)S(1)}, u32[]{:S(2)}, u32[]{:S(2)}) collective-permute-start(f32[4,128]{1,0:T(4,128)S(1)} %shard_map.130.first), channel_id=1, source_target_pairs={{0,9},{1,8},{2,11},{3,10},{4,13},{5,12},{6,15},{7,14},{8,1},{9,0},... | collective-permute-start | bytes 6152 | tf_op jit(solution)/shard_map/ppermute | solution.py:555
  79.7 3.9 %collective-permute-start.33 = (f32[4,128]{1,0:T(4,128)S(1)}, f32[4,128]{1,0:T(4,128)S(1)}, u32[]{:S(2)}, u32[]{:S(2)}) collective-permute-start(f32[4,128]{1,0:T(4,128)S(1)} %shard_map.131.packed), channel_id=1, source_target_pairs={{0,17},{1,16},{2,19},{3,18},{4,21},{5,20},{6,23},{7,22},{8,25},{9,... | collective-permute-start | bytes 6152 | tf_op jit(solution)/shard_map/ppermute | solution.py:555
  85.5 5.7 %collective-permute-start.36 = (f32[4,64,128]{2,1,0:T(8,128)S(1)}, f32[4,64,128]{2,1,0:T(8,128)S(1)}, u32[]{:S(2)}, u32[]{:S(2)}) collective-permute-start(f32[4,64,128]{2,1,0:T(8,128)S(1)} %wave_halo.29.cur.prev), channel_id=1, source_target_pairs={{0,4},{1,3},{2,6},{3,1},{4,0},{5,9},{6,2},{7,11},{8,12},{9,5},{10,... | collective-permute-start | bytes 393224 | tf_op jit(solution)/shard_map/ppermute | solution.py:551
  87.3 3.9 %collective-permute-start.37 = (f32[4,64,128]{2,1,0:T(8,128)S(1)}, f32[4,64,128]{2,1,0:T(8,128)S(1)}, u32[]{:S(2)}, u32[]{:S(2)}) collective-permute-start(f32[4,64,128]{2,1,0:T(8,128)S(1)} %wave_halo.29.cur.prev), channel_id=1, source_target_pairs={{0,1},{1,0},{2,3},{3,2},{4,5},{5,4},{6,7},{7,6},{8,9},{9,8},{10,11... | collective-permute-start | bytes 393224 | tf_op jit(solution)/shard_map/ppermute | solution.py:555
  91.3 5.5 %collective-permute-start.38 = (f32[4,64,128]{2,1,0:T(8,128)S(1)}, f32[4,64,128]{2,1,0:T(8,128)S(1)}, u32[]{:S(2)}, u32[]{:S(2)}) collective-permute-start(f32[4,64,128]{2,1,0:T(8,128)S(1)} %wave_halo.30.cur), channel_id=1, source_target_pairs={{0,4},{1,3},{2,6},{3,1},{4,0},{5,9},{6,2},{7,11},{8,12},{9,5},{10,... | collective-permute-start | bytes 393224 | tf_op jit(solution)/shard_map/ppermute | solution.py:551
  96.8 6.9 %collective-permute-start.43 = (f32[4,64,128]{2,1,0:T(8,128)S(1)}, f32[4,64,128]{2,1,0:T(8,128)S(1)}, u32[]{:S(2)}, u32[]{:S(2)}) collective-permute-start(f32[4,64,128]{2,1,0:T(8,128)S(1)} %wave_halo.31.cur.own), channel_id=1, source_target_pairs={{0,1},{1,0},{2,3},{3,2},{4,5},{5,4},{6,7},{7,6},{8,9},{9,8},{10,11... | collective-permute-start | bytes 393224 | tf_op jit(solution)/shard_map/ppermute | solution.py:555
  98.7 3.5 %collective-permute-start.41 = (f32[32,128]{1,0:T(8,128)S(1)}, f32[32,128]{1,0:T(8,128)S(1)}, u32[]{:S(2)}, u32[]{:S(2)}) collective-permute-start(f32[32,128]{1,0:T(8,128)S(1)} %shard_map.133.first), channel_id=1, source_target_pairs={{0,5},{1,4},{2,7},{3,6},{4,1},{5,0},{6,3},{7,2},{8,13},{9,12},{10,... | collective-permute-start | bytes 49160 | tf_op jit(solution)/shard_map/ppermute | solution.py:555
  102.2 3.2 %collective-permute-start.42 = (f32[32,128]{1,0:T(8,128)S(1)}, f32[32,128]{1,0:T(8,128)S(1)}, u32[]{:S(2)}, u32[]{:S(2)}) collective-permute-start(f32[32,128]{1,0:T(8,128)S(1)} %shard_map.134.first), channel_id=1, source_target_pairs={{0,9},{1,8},{2,11},{3,10},{4,13},{5,12},{6,15},{7,14},{8,1},{9,0},... | collective-permute-start | bytes 49160 | tf_op jit(solution)/shard_map/ppermute | solution.py:555
  105.3 4.2 %collective-permute-start.44 = (f32[32,128]{1,0:T(8,128)S(1)}, f32[32,128]{1,0:T(8,128)S(1)}, u32[]{:S(2)}, u32[]{:S(2)}) collective-permute-start(f32[32,128]{1,0:T(8,128)S(1)} %shard_map.135.packed), channel_id=1, source_target_pairs={{0,17},{1,16},{2,19},{3,18},{4,21},{5,20},{6,23},{7,22},{8,25},{9,... | collective-permute-start | bytes 49160 | tf_op jit(solution)/shard_map/ppermute | solution.py:555
  (16 other events, 75.7 us)

commit v3 on v1

--- a/solution.py
+++ b/solution.py
@@ -693,15 +693,15 @@
     hidden = chunks == 1 and count & (count - 1) == 0
     jobs = [exchange(1 << b) for b in range(stations.bit_length() - 1)]
     if hidden:
-        jobs += [build_table] + [forward(i) for i in range(pieces)] + [both(predict, cross)]
-        jobs += [add_up(1 << b) for b in range(count.bit_length() - 1)]
+        jobs += [build_table] + [forward(i) for i in range(pieces)] + [both(share_edges, predict)]
+        stages = [add_up(1 << b) for b in range(count.bit_length() - 1)]
+        jobs += [both(stages[0], cross)] + stages[1:]
         quarter = lines // 4
         jobs += [both(residual, adjoint(range(quarter)))]
         jobs += [adjoint(range(quarter, 3 * quarter)), adjoint(range(3 * quarter, lines))]
     jobs[0] = both(send_edges, jobs[0])
-    jobs[1] = both(share_edges, jobs[1])
     if not hidden:
-        jobs.append(cross)
+        jobs += [share_edges, cross]
     assert len(jobs) < steps
 
     surf = cour

time: 109 us -> 109 us (level)
    ppermute x28, waiting for transfers between devices: 12.5 us -> 11.1 us  [swap(): return lax.ppermute(value, AXES, pairs)]
where the time goes in v3:
time: 109 us
  starting transfers between devices  52 us (48%)
  Pallas kernels  29.3 us (27%)
  waiting for transfers between devices  25.5 us (23%)
  between operations  1.72 us (2%)
    ppermute x17, starting transfers between devices, across(): return lax.ppermute(value, AXES, chain)  36 us
    ppermute x28, starting transfers between devices, swap(): return lax.ppermute(value, AXES, pairs)  16 us
    ppermute x17, waiting for transfers between devices, across(): return lax.ppermute(value, AXES, chain)  14.3 us
    ppermute x28, waiting for transfers between devices, swap(): return lax.ppermute(value, AXES, pairs)  11.1 us
    pallas_call x5, Pallas kernels, gravity_forward(): pl.pallas_call(functools.partial(forward_kernel, first, guard, total_x, l...  9.5 us
    pallas_call x16, Pallas kernels, local_step(): pl.pallas_call(functools.partial(local_kernel, step), out_shape=(shape(cu...  6.24 us
    pallas_call x3, Pallas kernels, gravity_adjoint(): pl.pallas_call(functools.partial(adjoint_kernel, lines, guard, total_x, l...  5.05 us
  transfers between devices with their start and end apart: 45, of which 23 were waited for; matrix products, arithmetic and copies ran while one was open for 0% of the time, Pallas kernels for 25%

profile of v3, /device:TPU:0, one launch (start us, length us, event | category | flops | bytes accessed | tf_op | source)
XLA Modules:
  0.0 108.7 jit_solution(4292917867955573470)
XLA Ops:
  1.5 3.0 %collective-permute-start = (f32[4,64,128]{2,1,0:T(8,128)S(1)}, f32[4,64,128]{2,1,0:T(8,128)S(1)}, u32[]{:S(2)}, u32[]{:S(2)}) collective-permute-start(f32[4,64,128]{2,1,0:T(8,128)S(1)} %first_planes.1.cur.prev), channel_id=1, source_target_pairs={{0,4},{1,3},{2,6},{3,1},{4,0},{5,9},{6,2},{7,11},{8,12},{9,5},{10,... | collective-permute-start | bytes 393224 | tf_op jit(solution)/shard_map/ppermute | solution.py:551
  8.3 2.5 %collective-permute-start.2 = (f32[4,64,128]{2,1,0:T(8,128)S(1)}, f32[4,64,128]{2,1,0:T(8,128)S(1)}, u32[]{:S(2)}, u32[]{:S(2)}) collective-permute-start(f32[4,64,128]{2,1,0:T(8,128)S(1)} %wave_halo.16.cur.prev), channel_id=1, source_target_pairs={{0,4},{1,3},{2,6},{3,1},{4,0},{5,9},{6,2},{7,11},{8,12},{9,5},{10,... | collective-permute-start | bytes 393224 | tf_op jit(solution)/shard_map/ppermute | solution.py:551
  11.8 2.0 %collective-permute-done.2.outer = f32[4,64,128]{2,1,0:T(8,128)S(1)} collective-permute-done((f32[4,64,128]{2,1,0:T(8,128)S(1)}, f32[4,64,128]{2,1,0:T(8,128)S(1)}, u32[]{:S(2)}, u32[]{:S(2)}) %collective-permute-start.2) | collective-permute-done | bytes 131104 | tf_op jit(solution)/shard_map/ppermute | solution.py:551
  13.8 2.1 %collective-permute-start.5 = (f32[4,64,128]{2,1,0:T(8,128)S(1)}, f32[4,64,128]{2,1,0:T(8,128)S(1)}, u32[]{:S(2)}, u32[]{:S(2)}) collective-permute-start(f32[4,64,128]{2,1,0:T(8,128)S(1)} %wave_halo.17.cur.prev), channel_id=1, source_target_pairs={{0,4},{1,3},{2,6},{3,1},{4,0},{5,9},{6,2},{7,11},{8,12},{9,5},{10,... | collective-permute-start | bytes 393224 | tf_op jit(solution)/shard_map/ppermute | solution.py:551
  18.9 2.1 %collective-permute-start.8 = (f32[4,64,128]{2,1,0:T(8,128)S(1)}, f32[4,64,128]{2,1,0:T(8,128)S(1)}, u32[]{:S(2)}, u32[]{:S(2)}) collective-permute-start(f32[4,64,128]{2,1,0:T(8,128)S(1)} %wave_halo.18.cur.prev), channel_id=1, source_target_pairs={{0,4},{1,3},{2,6},{3,1},{4,0},{5,9},{6,2},{7,11},{8,12},{9,5},{10,... | collective-permute-start | bytes 393224 | tf_op jit(solution)/shard_map/ppermute | solution.py:551
  21.5 1.8 %gravity_table.1.table = f32[9088,128]{1,0:T(8,128)S(1)} custom-call(s32[1]{0:T(128)} %constant.54.clone.1.head), custom_call_target="tpu_custom_call" | custom-call | flops 23265280 | bytes 4653056 | tf_op jit(solution)/shard_map/gravity_table/pallas_call | solution.py:346
  24.0 2.1 %collective-permute-start.10 = (f32[4,64,128]{2,1,0:T(8,128)S(1)}, f32[4,64,128]{2,1,0:T(8,128)S(1)}, u32[]{:S(2)}, u32[]{:S(2)}) collective-permute-start(f32[4,64,128]{2,1,0:T(8,128)S(1)} %wave_halo.19.cur.prev), channel_id=1, source_target_pairs={{0,4},{1,3},{2,6},{3,1},{4,0},{5,9},{6,2},{7,11},{8,12},{9,5},{10,... | collective-permute-start | bytes 393224 | tf_op jit(solution)/shard_map/ppermute | solution.py:551
  26.5 1.9 %gravity_forward.5.refs_0_ = f32[104,128]{1,0:T(8,128)S(1)} custom-call(s32[513]{0:T(1024)S(1)} %pad_add_fusion.head, f32[9088,128]{1,0:T(8,128)S(1)} %gravity_table.1.table, f32[4,64,128]{2,1,0:T(8,128)S(1)} %get-tuple-element.141.dens), custom_call_target="tpu_custom_call" | custom-call | flops 13631488 | bytes 131072 | tf_op jit(solution)/shard_map/gravity_forward/pallas_call | solution.py:391
  29.1 2.1 %collective-permute-start.12 = (f32[4,64,128]{2,1,0:T(8,128)S(1)}, f32[4,64,128]{2,1,0:T(8,128)S(1)}, u32[]{:S(2)}, u32[]{:S(2)}) collective-permute-start(f32[4,64,128]{2,1,0:T(8,128)S(1)} %wave_halo.20.cur.prev), channel_id=1, source_target_pairs={{0,4},{1,3},{2,6},{3,1},{4,0},{5,9},{6,2},{7,11},{8,12},{9,5},{10,... | collective-permute-start | bytes 393224 | tf_op jit(solution)/shard_map/ppermute | solution.py:551
  31.6 1.9 %gravity_forward.6.refs_1_ = f32[104,128]{1,0:T(8,128)S(1)} custom-call(s32[513]{0:T(1024)S(1)} %pad_add_fusion.head, f32[9088,128]{1,0:T(8,128)S(1)} %gravity_table.1.table, f32[4,64,128]{2,1,0:T(8,128)S(1)} %get-tuple-element.141.dens), custom_call_target="tpu_custom_call" | custom-call | flops 13631488 | bytes 131072 | tf_op jit(solution)/shard_map/gravity_forward/pallas_call | solution.py:391
  34.2 2.1 %collective-permute-start.14 = (f32[4,64,128]{2,1,0:T(8,128)S(1)}, f32[4,64,128]{2,1,0:T(8,128)S(1)}, u32[]{:S(2)}, u32[]{:S(2)}) collective-permute-start(f32[4,64,128]{2,1,0:T(8,128)S(1)} %wave_halo.21.cur.prev), channel_id=1, source_target_pairs={{0,4},{1,3},{2,6},{3,1},{4,0},{5,9},{6,2},{7,11},{8,12},{9,5},{10,... | collective-permute-start | bytes 393224 | tf_op jit(solution)/shard_map/ppermute | solution.py:551
  36.7 1.9 %gravity_forward.7.refs_2_ = f32[104,128]{1,0:T(8,128)S(1)} custom-call(s32[513]{0:T(1024)S(1)} %pad_add_fusion.head, f32[9088,128]{1,0:T(8,128)S(1)} %gravity_table.1.table, f32[4,64,128]{2,1,0:T(8,128)S(1)} %get-tuple-element.141.dens), custom_call_target="tpu_custom_call" | custom-call | flops 13631488 | bytes 131072 | tf_op jit(solution)/shard_map/gravity_forward/pallas_call | solution.py:391
  39.3 2.1 %collective-permute-start.16 = (f32[4,64,128]{2,1,0:T(8,128)S(1)}, f32[4,64,128]{2,1,0:T(8,128)S(1)}, u32[]{:S(2)}, u32[]{:S(2)}) collective-permute-start(f32[4,64,128]{2,1,0:T(8,128)S(1)} %wave_halo.22.cur.prev), channel_id=1, source_target_pairs={{0,4},{1,3},{2,6},{3,1},{4,0},{5,9},{6,2},{7,11},{8,12},{9,5},{10,... | collective-permute-start | bytes 393224 | tf_op jit(solution)/shard_map/ppermute | solution.py:551
  41.8 1.9 %gravity_forward.8.refs_3_ = f32[104,128]{1,0:T(8,128)S(1)} custom-call(s32[513]{0:T(1024)S(1)} %pad_add_fusion.head, f32[9088,128]{1,0:T(8,128)S(1)} %gravity_table.1.table, f32[4,64,128]{2,1,0:T(8,128)S(1)} %get-tuple-element.141.dens), custom_call_target="tpu_custom_call" | custom-call | flops 13631488 | bytes 131072 | tf_op jit(solution)/shard_map/gravity_forward/pallas_call | solution.py:391
  44.5 2.1 %collective-permute-start.18 = (f32[4,64,128]{2,1,0:T(8,128)S(1)}, f32[4,64,128]{2,1,0:T(8,128)S(1)}, u32[]{:S(2)}, u32[]{:S(2)}) collective-permute-start(f32[4,64,128]{2,1,0:T(8,128)S(1)} %wave_halo.23.cur.prev), channel_id=1, source_target_pairs={{0,4},{1,3},{2,6},{3,1},{4,0},{5,9},{6,2},{7,11},{8,12},{9,5},{10,... | collective-permute-start | bytes 393224 | tf_op jit(solution)/shard_map/ppermute | solution.py:551
  46.9 1.8 %gravity_forward.9.refs_4_ = f32[96,128]{1,0:T(8,128)S(1)} custom-call(s32[513]{0:T(1024)S(1)} %pad_add_fusion.head, f32[9088,128]{1,0:T(8,128)S(1)} %gravity_table.1.table, f32[4,64,128]{2,1,0:T(8,128)S(1)} %get-tuple-element.141.dens), custom_call_target="tpu_custom_call" | custom-call | flops 12582912 | bytes 131072 | tf_op jit(solution)/shard_map/gravity_forward/pallas_call | solution.py:391
  49.6 2.2 %collective-permute-start.21 = (f32[4,64,128]{2,1,0:T(8,128)S(1)}, f32[4,64,128]{2,1,0:T(8,128)S(1)}, u32[]{:S(2)}, u32[]{:S(2)}) collective-permute-start(f32[4,64,128]{2,1,0:T(8,128)S(1)} %wave_halo.24.cur.prev), channel_id=1, source_target_pairs={{0,4},{1,3},{2,6},{3,1},{4,0},{5,9},{6,2},{7,11},{8,12},{9,5},{10,... | collective-permute-start | bytes 393224 | tf_op jit(solution)/shard_map/ppermute | solution.py:551
  53.0 2.9 %collective-permute-done.20.outer = f32[2,64,128]{2,1,0:T(8,128)S(1)} collective-permute-done((f32[2,64,128]{2,1,0:T(8,128)S(1)}, f32[2,64,128]{2,1,0:T(8,128)S(1)}, u32[]{:S(2)}, u32[]{:S(2)}) %collective-permute-start.20) | collective-permute-done | bytes 65568 | tf_op jit(solution)/shard_map/ppermute | solution.py:551
  56.1 2.2 %collective-permute-start.24 = (f32[4,64,128]{2,1,0:T(8,128)S(1)}, f32[4,64,128]{2,1,0:T(8,128)S(1)}, u32[]{:S(2)}, u32[]{:S(2)}) collective-permute-start(f32[4,64,128]{2,1,0:T(8,128)S(1)} %wave_halo.25.cur.prev), channel_id=1, source_target_pairs={{0,4},{1,3},{2,6},{3,1},{4,0},{5,9},{6,2},{7,11},{8,12},{9,5},{10,... | collective-permute-start | bytes 393224 | tf_op jit(solution)/shard_map/ppermute | solution.py:551
  61.2 2.5 %collective-permute-start.27 = (f32[4,64,128]{2,1,0:T(8,128)S(1)}, f32[4,64,128]{2,1,0:T(8,128)S(1)}, u32[]{:S(2)}, u32[]{:S(2)}) collective-permute-start(f32[4,64,128]{2,1,0:T(8,128)S(1)} %wave_halo.26.cur.prev), channel_id=1, source_target_pairs={{0,4},{1,3},{2,6},{3,1},{4,0},{5,9},{6,2},{7,11},{8,12},{9,5},{10,... | collective-permute-start | bytes 393224 | tf_op jit(solution)/shard_map/ppermute | solution.py:551
  66.7 2.2 %collective-permute-start.30 = (f32[4,64,128]{2,1,0:T(8,128)S(1)}, f32[4,64,128]{2,1,0:T(8,128)S(1)}, u32[]{:S(2)}, u32[]{:S(2)}) collective-permute-start(f32[4,64,128]{2,1,0:T(8,128)S(1)} %wave_halo.27.cur.prev), channel_id=1, source_target_pairs={{0,4},{1,3},{2,6},{3,1},{4,0},{5,9},{6,2},{7,11},{8,12},{9,5},{10,... | collective-permute-start | bytes 393224 | tf_op jit(solution)/shard_map/ppermute | solution.py:551
  69.2 2.8 %collective-permute-done.29.second = f32[4,128]{1,0:T(4,128)S(1)} collective-permute-done((f32[4,128]{1,0:T(4,128)S(1)}, f32[4,128]{1,0:T(4,128)S(1)}, u32[]{:S(2)}, u32[]{:S(2)}) %collective-permute-start.29) | collective-permute-done | bytes 2080 | tf_op jit(solution)/shard_map/ppermute | solution.py:555
  74.3 2.2 %collective-permute-start.32 = (f32[4,128]{1,0:T(4,128)S(1)}, f32[4,128]{1,0:T(4,128)S(1)}, u32[]{:S(2)}, u32[]{:S(2)}) collective-permute-start(f32[4,128]{1,0:T(4,128)S(1)} %shard_map.130.first), channel_id=1, source_target_pairs={{0,9},{1,8},{2,11},{3,10},{4,13},{5,12},{6,15},{7,14},{8,1},{9,0},... | collective-permute-start | bytes 6152 | tf_op jit(solution)/shard_map/ppermute | solution.py:555
  76.5 1.7 %collective-permute-done.32.second = f32[4,128]{1,0:T(4,128)S(1)} collective-permute-done((f32[4,128]{1,0:T(4,128)S(1)}, f32[4,128]{1,0:T(4,128)S(1)}, u32[]{:S(2)}, u32[]{:S(2)}) %collective-permute-start.32) | collective-permute-done | bytes 2080 | tf_op jit(solution)/shard_map/ppermute | solution.py:555
  78.2 2.6 %collective-permute-start.33 = (f32[4,128]{1,0:T(4,128)S(1)}, f32[4,128]{1,0:T(4,128)S(1)}, u32[]{:S(2)}, u32[]{:S(2)}) collective-permute-start(f32[4,128]{1,0:T(4,128)S(1)} %shard_map.131.packed), channel_id=1, source_target_pairs={{0,17},{1,16},{2,19},{3,18},{4,21},{5,20},{6,23},{7,22},{8,25},{9,... | collective-permute-start | bytes 6152 | tf_op jit(solution)/shard_map/ppermute | solution.py:555
  84.0 1.7 %collective-permute-start.36 = (f32[4,64,128]{2,1,0:T(8,128)S(1)}, f32[4,64,128]{2,1,0:T(8,128)S(1)}, u32[]{:S(2)}, u32[]{:S(2)}) collective-permute-start(f32[4,64,128]{2,1,0:T(8,128)S(1)} %wave_halo.29.cur.prev), channel_id=1, source_target_pairs={{0,4},{1,3},{2,6},{3,1},{4,0},{5,9},{6,2},{7,11},{8,12},{9,5},{10,... | collective-permute-start | bytes 393224 | tf_op jit(solution)/shard_map/ppermute | solution.py:551
  86.4 1.9 %gravity_adjoint.4.start_at = f32[8,16,128]{2,1,0:T(8,128)S(1)} custom-call(s32[513]{0:T(1024)S(1)} %pad_add_fusion.head, f32[4,128]{1,0:T(4,128)S(1)} %get-tuple-element.208.weights, f32[9088,128]{1,0:T(8,128)S(1)} %gravity_table.1.table, f32[8,16,128]{2,1,0:T(8,128)S(1)} %gravity_adjoint.3.start_at), custom_call_target="tpu_custom_call" | custom-call | flops 8388608 | bytes 131072 | tf_op jit(solution)/shard_map/gravity_adjoint/pallas_call | solution.py:431
  89.7 2.5 %collective-permute-start.38 = (f32[4,64,128]{2,1,0:T(8,128)S(1)}, f32[4,64,128]{2,1,0:T(8,128)S(1)}, u32[]{:S(2)}, u32[]{:S(2)}) collective-permute-start(f32[4,64,128]{2,1,0:T(8,128)S(1)} %wave_halo.30.cur), channel_id=1, source_target_pairs={{0,4},{1,3},{2,6},{3,1},{4,0},{5,9},{6,2},{7,11},{8,12},{9,5},{10,... | collective-permute-start | bytes 393224 | tf_op jit(solution)/shard_map/ppermute | solution.py:551
  92.6 1.9 %gravity_adjoint.5 = f32[8,16,128]{2,1,0:T(8,128)} custom-call(s32[513]{0:T(1024)S(1)} %pad_add_fusion.head, f32[4,128]{1,0:T(4,128)S(1)} %get-tuple-element.208.weights, f32[9088,128]{1,0:T(8,128)S(1)} %gravity_table.1.table, f32[8,16,128]{2,1,0:T(8,128)S(1)} %gravity_adjoint.4.start_at), custom_call_target="tpu_custom_call" | custom-call | flops 4194304 | bytes 131072 | tf_op jit(solution)/shard_map/gravity_adjoint/pallas_call | solution.py:431
  97.1 2.0 %collective-permute-start.41 = (f32[32,128]{1,0:T(8,128)S(1)}, f32[32,128]{1,0:T(8,128)S(1)}, u32[]{:S(2)}, u32[]{:S(2)}) collective-permute-start(f32[32,128]{1,0:T(8,128)S(1)} %shard_map.133.first), channel_id=1, source_target_pairs={{0,5},{1,4},{2,7},{3,6},{4,1},{5,0},{6,3},{7,2},{8,13},{9,12},{10,... | collective-permute-start | bytes 49160 | tf_op jit(solution)/shard_map/ppermute | solution.py:555
  100.6 1.7 %collective-permute-start.42 = (f32[32,128]{1,0:T(8,128)S(1)}, f32[32,128]{1,0:T(8,128)S(1)}, u32[]{:S(2)}, u32[]{:S(2)}) collective-permute-start(f32[32,128]{1,0:T(8,128)S(1)} %shard_map.134.first), channel_id=1, source_target_pairs={{0,9},{1,8},{2,11},{3,10},{4,13},{5,12},{6,15},{7,14},{8,1},{9,0},... | collective-permute-start | bytes 49160 | tf_op jit(solution)/shard_map/ppermute | solution.py:555
  103.7 2.9 %collective-permute-start.44 = (f32[32,128]{1,0:T(8,128)S(1)}, f32[32,128]{1,0:T(8,128)S(1)}, u32[]{:S(2)}, u32[]{:S(2)}) collective-permute-start(f32[32,128]{1,0:T(8,128)S(1)} %shard_map.135.packed), channel_id=1, source_target_pairs={{0,17},{1,16},{2,19},{3,18},{4,21},{5,20},{6,23},{7,22},{8,25},{9,... | collective-permute-start | bytes 49160 | tf_op jit(solution)/shard_map/ppermute | solution.py:555
  (126 shorter events, 37.5 us)
Async XLA Ops:
  1.5 6.7 %collective-permute-start = (f32[4,64,128]{2,1,0:T(8,128)S(1)}, f32[4,64,128]{2,1,0:T(8,128)S(1)}, u32[]{:S(2)}, u32[]{:S(2)}) collective-permute-start(f32[4,64,128]{2,1,0:T(8,128)S(1)} %first_planes.1.cur.prev), channel_id=1, source_target_pairs={{0,4},{1,3},{2,6},{3,1},{4,0},{5,9},{6,2},{7,11},{8,12},{9,5},{10,... | collective-permute-start | bytes 393224 | tf_op jit(solution)/shard_map/ppermute | solution.py:551
  4.5 3.7 %collective-permute-start.1 = (f32[4,64,128]{2,1,0:T(8,128)S(1)}, f32[4,64,128]{2,1,0:T(8,128)S(1)}, u32[]{:S(2)}, u32[]{:S(2)}) collective-permute-start(f32[4,64,128]{2,1,0:T(8,128)S(1)} %first_planes.1.cur.prev), channel_id=1, source_target_pairs={{0,1},{1,0},{2,3},{3,2},{4,5},{5,4},{6,7},{7,6},{8,9},{9,8},{10,11... | collective-permute-start | bytes 393224 | tf_op jit(solution)/shard_map/ppermute | solution.py:555
  8.3 5.5 %collective-permute-start.2 = (f32[4,64,128]{2,1,0:T(8,128)S(1)}, f32[4,64,128]{2,1,0:T(8,128)S(1)}, u32[]{:S(2)}, u32[]{:S(2)}) collective-permute-start(f32[4,64,128]{2,1,0:T(8,128)S(1)} %wave_halo.16.cur.prev), channel_id=1, source_target_pairs={{0,4},{1,3},{2,6},{3,1},{4,0},{5,9},{6,2},{7,11},{8,12},{9,5},{10,... | collective-permute-start | bytes 393224 | tf_op jit(solution)/shard_map/ppermute | solution.py:551
  10.8 3.0 %collective-permute-start.3 = (f32[4,64,128]{2,1,0:T(8,128)S(1)}, f32[4,64,128]{2,1,0:T(8,128)S(1)}, u32[]{:S(2)}, u32[]{:S(2)}) collective-permute-start(f32[4,64,128]{2,1,0:T(8,128)S(1)} %wave_halo.16.cur.prev), channel_id=1, source_target_pairs={{0,1},{1,0},{2,3},{3,2},{4,5},{5,4},{6,7},{7,6},{8,9},{9,8},{10,11... | collective-permute-start | bytes 393224 | tf_op jit(solution)/shard_map/ppermute | solution.py:555
  11.2 5.1 %collective-permute-start.4 = (f32[2,1,128]{2,1,0:T(1,128)S(1)}, f32[2,1,128]{2,1,0:T(1,128)S(1)}, u32[]{:S(2)}, u32[]{:S(2)}) collective-permute-start(f32[2,1,128]{2,1,0:T(1,128)S(1)} %get-tuple-element.125), channel_id=1, source_target_pairs={{0,1},{1,0},{2,3},{3,2},{4,5},{5,4},{6,7},{7,6},{8,9},{9,8},{10,11... | collective-permute-start | bytes 3080 | tf_op jit(solution)/shard_map/ppermute | solution.py:555
  13.8 5.0 %collective-permute-start.5 = (f32[4,64,128]{2,1,0:T(8,128)S(1)}, f32[4,64,128]{2,1,0:T(8,128)S(1)}, u32[]{:S(2)}, u32[]{:S(2)}) collective-permute-start(f32[4,64,128]{2,1,0:T(8,128)S(1)} %wave_halo.17.cur.prev), channel_id=1, source_target_pairs={{0,4},{1,3},{2,6},{3,1},{4,0},{5,9},{6,2},{7,11},{8,12},{9,5},{10,... | collective-permute-start | bytes 393224 | tf_op jit(solution)/shard_map/ppermute | solution.py:551
  16.4 5.1 %collective-permute-start.7 = (f32[2,2,128]{2,1,0:T(2,128)S(1)}, f32[2,2,128]{2,1,0:T(2,128)S(1)}, u32[]{:S(2)}, u32[]{:S(2)}) collective-permute-start(f32[2,2,128]{2,1,0:T(2,128)S(1)} %pad_maximum_fusion.1), channel_id=1, source_target_pairs={{0,2},{1,3},{2,0},{3,1},{4,6},{5,7},{6,4},{7,5},{8,10},{9,11},{10,... | collective-permute-start | bytes 6152 | tf_op jit(solution)/shard_map/ppermute | solution.py:555
  18.9 5.0 %collective-permute-start.8 = (f32[4,64,128]{2,1,0:T(8,128)S(1)}, f32[4,64,128]{2,1,0:T(8,128)S(1)}, u32[]{:S(2)}, u32[]{:S(2)}) collective-permute-start(f32[4,64,128]{2,1,0:T(8,128)S(1)} %wave_halo.18.cur.prev), channel_id=1, source_target_pairs={{0,4},{1,3},{2,6},{3,1},{4,0},{5,9},{6,2},{7,11},{8,12},{9,5},{10,... | collective-permute-start | bytes 393224 | tf_op jit(solution)/shard_map/ppermute | solution.py:551
  24.0 5.0 %collective-permute-start.10 = (f32[4,64,128]{2,1,0:T(8,128)S(1)}, f32[4,64,128]{2,1,0:T(8,128)S(1)}, u32[]{:S(2)}, u32[]{:S(2)}) collective-permute-start(f32[4,64,128]{2,1,0:T(8,128)S(1)} %wave_halo.19.cur.prev), channel_id=1, source_target_pairs={{0,4},{1,3},{2,6},{3,1},{4,0},{5,9},{6,2},{7,11},{8,12},{9,5},{10,... | collective-permute-start | bytes 393224 | tf_op jit(solution)/shard_map/ppermute | solution.py:551
  29.1 5.0 %collective-permute-start.12 = (f32[4,64,128]{2,1,0:T(8,128)S(1)}, f32[4,64,128]{2,1,0:T(8,128)S(1)}, u32[]{:S(2)}, u32[]{:S(2)}) collective-permute-start(f32[4,64,128]{2,1,0:T(8,128)S(1)} %wave_halo.20.cur.prev), channel_id=1, source_target_pairs={{0,4},{1,3},{2,6},{3,1},{4,0},{5,9},{6,2},{7,11},{8,12},{9,5},{10,... | collective-permute-start | bytes 393224 | tf_op jit(solution)/shard_map/ppermute | solution.py:551
  34.2 5.0 %collective-permute-start.14 = (f32[4,64,128]{2,1,0:T(8,128)S(1)}, f32[4,64,128]{2,1,0:T(8,128)S(1)}, u32[]{:S(2)}, u32[]{:S(2)}) collective-permute-start(f32[4,64,128]{2,1,0:T(8,128)S(1)} %wave_halo.21.cur.prev), channel_id=1, source_target_pairs={{0,4},{1,3},{2,6},{3,1},{4,0},{5,9},{6,2},{7,11},{8,12},{9,5},{10,... | collective-permute-start | bytes 393224 | tf_op jit(solution)/shard_map/ppermute | solution.py:551
  39.3 5.0 %collective-permute-start.16 = (f32[4,64,128]{2,1,0:T(8,128)S(1)}, f32[4,64,128]{2,1,0:T(8,128)S(1)}, u32[]{:S(2)}, u32[]{:S(2)}) collective-permute-start(f32[4,64,128]{2,1,0:T(8,128)S(1)} %wave_halo.22.cur.prev), channel_id=1, source_target_pairs={{0,4},{1,3},{2,6},{3,1},{4,0},{5,9},{6,2},{7,11},{8,12},{9,5},{10,... | collective-permute-start | bytes 393224 | tf_op jit(solution)/shard_map/ppermute | solution.py:551
  44.5 5.0 %collective-permute-start.18 = (f32[4,64,128]{2,1,0:T(8,128)S(1)}, f32[4,64,128]{2,1,0:T(8,128)S(1)}, u32[]{:S(2)}, u32[]{:S(2)}) collective-permute-start(f32[4,64,128]{2,1,0:T(8,128)S(1)} %wave_halo.23.cur.prev), channel_id=1, source_target_pairs={{0,4},{1,3},{2,6},{3,1},{4,0},{5,9},{6,2},{7,11},{8,12},{9,5},{10,... | collective-permute-start | bytes 393224 | tf_op jit(solution)/shard_map/ppermute | solution.py:551
  49.6 6.4 %collective-permute-start.21 = (f32[4,64,128]{2,1,0:T(8,128)S(1)}, f32[4,64,128]{2,1,0:T(8,128)S(1)}, u32[]{:S(2)}, u32[]{:S(2)}) collective-permute-start(f32[4,64,128]{2,1,0:T(8,128)S(1)} %wave_halo.24.cur.prev), channel_id=1, source_target_pairs={{0,4},{1,3},{2,6},{3,1},{4,0},{5,9},{6,2},{7,11},{8,12},{9,5},{10,... | collective-permute-start | bytes 393224 | tf_op jit(solution)/shard_map/ppermute | solution.py:551
  51.7 4.3 %collective-permute-start.22 = (f32[4,64,128]{2,1,0:T(8,128)S(1)}, f32[4,64,128]{2,1,0:T(8,128)S(1)}, u32[]{:S(2)}, u32[]{:S(2)}) collective-permute-start(f32[4,64,128]{2,1,0:T(8,128)S(1)} %wave_halo.24.cur.prev), channel_id=1, source_target_pairs={{0,1},{1,0},{2,3},{3,2},{4,5},{5,4},{6,7},{7,6},{8,9},{9,8},{10,11... | collective-permute-start | bytes 393224 | tf_op jit(solution)/shard_map/ppermute | solution.py:555
  51.7 4.3 %collective-permute-start.20 = (f32[2,64,128]{2,1,0:T(8,128)S(1)}, f32[2,64,128]{2,1,0:T(8,128)S(1)}, u32[]{:S(2)}, u32[]{:S(2)}) collective-permute-start(f32[2,64,128]{2,1,0:T(8,128)S(1)} %get-tuple-element.165), channel_id=1, source_target_pairs={{0,4},{1,3},{2,6},{3,1},{4,0},{5,9},{6,2},{7,11},{8,12},{9,5},{10,... | collective-permute-start | bytes 196616 | tf_op jit(solution)/shard_map/ppermute | solution.py:551
  56.1 5.1 %collective-permute-start.24 = (f32[4,64,128]{2,1,0:T(8,128)S(1)}, f32[4,64,128]{2,1,0:T(8,128)S(1)}, u32[]{:S(2)}, u32[]{:S(2)}) collective-permute-start(f32[4,64,128]{2,1,0:T(8,128)S(1)} %wave_halo.25.cur.prev), channel_id=1, source_target_pairs={{0,4},{1,3},{2,6},{3,1},{4,0},{5,9},{6,2},{7,11},{8,12},{9,5},{10,... | collective-permute-start | bytes 393224 | tf_op jit(solution)/shard_map/ppermute | solution.py:551
  61.2 5.4 %collective-permute-start.27 = (f32[4,64,128]{2,1,0:T(8,128)S(1)}, f32[4,64,128]{2,1,0:T(8,128)S(1)}, u32[]{:S(2)}, u32[]{:S(2)}) collective-permute-start(f32[4,64,128]{2,1,0:T(8,128)S(1)} %wave_halo.26.cur.prev), channel_id=1, source_target_pairs={{0,4},{1,3},{2,6},{3,1},{4,0},{5,9},{6,2},{7,11},{8,12},{9,5},{10,... | collective-permute-start | bytes 393224 | tf_op jit(solution)/shard_map/ppermute | solution.py:551
  66.7 5.6 %collective-permute-start.30 = (f32[4,64,128]{2,1,0:T(8,128)S(1)}, f32[4,64,128]{2,1,0:T(8,128)S(1)}, u32[]{:S(2)}, u32[]{:S(2)}) collective-permute-start(f32[4,64,128]{2,1,0:T(8,128)S(1)} %wave_halo.27.cur.prev), channel_id=1, source_target_pairs={{0,4},{1,3},{2,6},{3,1},{4,0},{5,9},{6,2},{7,11},{8,12},{9,5},{10,... | collective-permute-start | bytes 393224 | tf_op jit(solution)/shard_map/ppermute | solution.py:551
  69.0 3.4 %collective-permute-start.31 = (f32[4,64,128]{2,1,0:T(8,128)S(1)}, f32[4,64,128]{2,1,0:T(8,128)S(1)}, u32[]{:S(2)}, u32[]{:S(2)}) collective-permute-start(f32[4,64,128]{2,1,0:T(8,128)S(1)} %wave_halo.27.cur.prev), channel_id=1, source_target_pairs={{0,1},{1,0},{2,3},{3,2},{4,5},{5,4},{6,7},{7,6},{8,9},{9,8},{10,11... | collective-permute-start | bytes 393224 | tf_op jit(solution)/shard_map/ppermute | solution.py:555
  69.0 3.0 %collective-permute-start.29 = (f32[4,128]{1,0:T(4,128)S(1)}, f32[4,128]{1,0:T(4,128)S(1)}, u32[]{:S(2)}, u32[]{:S(2)}) collective-permute-start(f32[4,128]{1,0:T(4,128)S(1)} %shard_map.129.first), channel_id=1, source_target_pairs={{0,5},{1,4},{2,7},{3,6},{4,1},{5,0},{6,3},{7,2},{8,13},{9,12},{10,... | collective-permute-start | bytes 6152 | tf_op jit(solution)/shard_map/ppermute | solution.py:555
  72.5 11.4 %collective-permute-start.34 = (f32[4,64,128]{2,1,0:T(8,128)S(1)}, f32[4,64,128]{2,1,0:T(8,128)S(1)}, u32[]{:S(2)}, u32[]{:S(2)}) collective-permute-start(f32[4,64,128]{2,1,0:T(8,128)S(1)} %wave_halo.28.cur.prev), channel_id=1, source_target_pairs={{0,4},{1,3},{2,6},{3,1},{4,0},{5,9},{6,2},{7,11},{8,12},{9,5},{10,... | collective-permute-start | bytes 393224 | tf_op jit(solution)/shard_map/ppermute | solution.py:551
  74.1 9.8 %collective-permute-start.35 = (f32[4,64,128]{2,1,0:T(8,128)S(1)}, f32[4,64,128]{2,1,0:T(8,128)S(1)}, u32[]{:S(2)}, u32[]{:S(2)}) collective-permute-start(f32[4,64,128]{2,1,0:T(8,128)S(1)} %wave_halo.28.cur.prev), channel_id=1, source_target_pairs={{0,1},{1,0},{2,3},{3,2},{4,5},{5,4},{6,7},{7,6},{8,9},{9,8},{10,11... | collective-permute-start | bytes 393224 | tf_op jit(solution)/shard_map/ppermute | solution.py:555
  74.3 3.9 %collective-permute-start.32 = (f32[4,128]{1,0:T(4,128)S(1)}, f32[4,128]{1,0:T(4,128)S(1)}, u32[]{:S(2)}, u32[]{:S(2)}) collective-permute-start(f32[4,128]{1,0:T(4,128)S(1)} %shard_map.130.first), channel_id=1, source_target_pairs={{0,9},{1,8},{2,11},{3,10},{4,13},{5,12},{6,15},{7,14},{8,1},{9,0},... | collective-permute-start | bytes 6152 | tf_op jit(solution)/shard_map/ppermute | solution.py:555
  78.2 4.0 %collective-permute-start.33 = (f32[4,128]{1,0:T(4,128)S(1)}, f32[4,128]{1,0:T(4,128)S(1)}, u32[]{:S(2)}, u32[]{:S(2)}) collective-permute-start(f32[4,128]{1,0:T(4,128)S(1)} %shard_map.131.packed), channel_id=1, source_target_pairs={{0,17},{1,16},{2,19},{3,18},{4,21},{5,20},{6,23},{7,22},{8,25},{9,... | collective-permute-start | bytes 6152 | tf_op jit(solution)/shard_map/ppermute | solution.py:555
  84.0 5.6 %collective-permute-start.36 = (f32[4,64,128]{2,1,0:T(8,128)S(1)}, f32[4,64,128]{2,1,0:T(8,128)S(1)}, u32[]{:S(2)}, u32[]{:S(2)}) collective-permute-start(f32[4,64,128]{2,1,0:T(8,128)S(1)} %wave_halo.29.cur.prev), channel_id=1, source_target_pairs={{0,4},{1,3},{2,6},{3,1},{4,0},{5,9},{6,2},{7,11},{8,12},{9,5},{10,... | collective-permute-start | bytes 393224 | tf_op jit(solution)/shard_map/ppermute | solution.py:551
  85.7 3.9 %collective-permute-start.37 = (f32[4,64,128]{2,1,0:T(8,128)S(1)}, f32[4,64,128]{2,1,0:T(8,128)S(1)}, u32[]{:S(2)}, u32[]{:S(2)}) collective-permute-start(f32[4,64,128]{2,1,0:T(8,128)S(1)} %wave_halo.29.cur.prev), channel_id=1, source_target_pairs={{0,1},{1,0},{2,3},{3,2},{4,5},{5,4},{6,7},{7,6},{8,9},{9,8},{10,11... | collective-permute-start | bytes 393224 | tf_op jit(solution)/shard_map/ppermute | solution.py:555
  89.7 5.5 %collective-permute-start.38 = (f32[4,64,128]{2,1,0:T(8,128)S(1)}, f32[4,64,128]{2,1,0:T(8,128)S(1)}, u32[]{:S(2)}, u32[]{:S(2)}) collective-permute-start(f32[4,64,128]{2,1,0:T(8,128)S(1)} %wave_halo.30.cur), channel_id=1, source_target_pairs={{0,4},{1,3},{2,6},{3,1},{4,0},{5,9},{6,2},{7,11},{8,12},{9,5},{10,... | collective-permute-start | bytes 393224 | tf_op jit(solution)/shard_map/ppermute | solution.py:551
  95.2 7.0 %collective-permute-start.43 = (f32[4,64,128]{2,1,0:T(8,128)S(1)}, f32[4,64,128]{2,1,0:T(8,128)S(1)}, u32[]{:S(2)}, u32[]{:S(2)}) collective-permute-start(f32[4,64,128]{2,1,0:T(8,128)S(1)} %wave_halo.31.cur.own), channel_id=1, source_target_pairs={{0,1},{1,0},{2,3},{3,2},{4,5},{5,4},{6,7},{7,6},{8,9},{9,8},{10,11... | collective-permute-start | bytes 393224 | tf_op jit(solution)/shard_map/ppermute | solution.py:555
  97.1 3.5 %collective-permute-start.41 = (f32[32,128]{1,0:T(8,128)S(1)}, f32[32,128]{1,0:T(8,128)S(1)}, u32[]{:S(2)}, u32[]{:S(2)}) collective-permute-start(f32[32,128]{1,0:T(8,128)S(1)} %shard_map.133.first), channel_id=1, source_target_pairs={{0,5},{1,4},{2,7},{3,6},{4,1},{5,0},{6,3},{7,2},{8,13},{9,12},{10,... | collective-permute-start | bytes 49160 | tf_op jit(solution)/shard_map/ppermute | solution.py:555
  100.6 3.2 %collective-permute-start.42 = (f32[32,128]{1,0:T(8,128)S(1)}, f32[32,128]{1,0:T(8,128)S(1)}, u32[]{:S(2)}, u32[]{:S(2)}) collective-permute-start(f32[32,128]{1,0:T(8,128)S(1)} %shard_map.134.first), channel_id=1, source_target_pairs={{0,9},{1,8},{2,11},{3,10},{4,13},{5,12},{6,15},{7,14},{8,1},{9,0},... | collective-permute-start | bytes 49160 | tf_op jit(solution)/shard_map/ppermute | solution.py:555
  103.7 4.3 %collective-permute-start.44 = (f32[32,128]{1,0:T(8,128)S(1)}, f32[32,128]{1,0:T(8,128)S(1)}, u32[]{:S(2)}, u32[]{:S(2)}) collective-permute-start(f32[32,128]{1,0:T(8,128)S(1)} %shard_map.135.packed), channel_id=1, source_target_pairs={{0,17},{1,16},{2,19},{3,18},{4,21},{5,20},{6,23},{7,22},{8,25},{9,... | collective-permute-start | bytes 49160 | tf_op jit(solution)/shard_map/ppermute | solution.py:555
  (16 other events, 82.8 us)
